TPU v7x, 32 devices: a whole 2x2x4 slice. The times are simulated.
32 devices in a mesh: groups: 2 (over x), att: 2 (over y), exp: 8 (over z, core).
Axes of the slice: x: 2, y: 2, z: 4, core: 2. Of those that a mesh axis runs over, the one named last changes fastest.
Arguments:
- queries: bfloat16 [1024, 4096], P(('groups', 'exp')), parts along dimension 0, may hold values from -12 to 12
- row_key_value: bfloat16 [1024, 1024], P(('groups', 'exp')), parts along dimension 0, may hold values from -12 to 12
- shared_context_cache: bfloat16 [4, 1024, 1024], P('groups', 'att'), parts along dimension 0, may hold values from -6 to 6
- branch: int32 [1024], P(('groups', 'exp')), parts along dimension 0, may hold values from 0 to 1
- sink_logits: float32 [64], replicated, may hold values from 8 to 13
- w_out: bfloat16 [4096, 2880], P(None, 'att'), may hold values from -0.09375 to 0.09375
- residual: bfloat16 [1024, 2880], P(('groups', 'exp'), 'att'), parts along dimension 0, may hold values from -20 to 20
- norm_gain: bfloat16 [2880], P('att'), may hold values from 0.099609375 to 1.8984375
- expert_ids: int32 [1024, 4], P(('groups', 'exp')), parts along dimension 0, may hold values from 0 to 7, all different within a row; in each aligned block of 64 rows (0 to 63, 64 to 127, ...) at most 64 rows name the same one
- weight_codes: int32 [1024, 4], P(('groups', 'exp')), parts along dimension 0, may hold values from 1 to 255
- w_gate: bfloat16 [8, 2880, 2880], P('exp', None, 'att'), may hold values from -0.4375 to 0.4375
- w_up: bfloat16 [8, 2880, 2880], P('exp', None, 'att'), may hold values from -0.4375 to 0.4375
- w_down: bfloat16 [8, 2880, 2880], P('exp', 'att'), may hold values from -0.013671875 to 0.013671875
Outputs:
- attended: bfloat16 [1024, 2880], P(('groups', 'exp'), 'att'), parts along dimension 0
- expert_mix: bfloat16 [1024, 2880], P(('groups', 'exp'), 'att'), parts along dimension 0
There are 2 independent parts, one for each index of `groups`. A program takes and returns all parts, laid end to end along the dimension named above; an argument that names none is the same for every part. Nothing has to cross between parts.
Inputs may be any that keep to these rules, and one draw needn't show every extreme that they name: `expert_ids`: each row names 4 different experts; within the rows of one index of exp (aligned blocks of 64 rows) no expert is named more than 64 times, and in some block some expert is named exactly 64 times.
All inputs are finite; a program needn't handle non-finite values.
Results may differ from a plain program's by a relative error of at most 0.022.
Values may be sent and summed in bfloat16 or wider, within the bound.
A program may use at most 128 MiB of HBM per device.

v0:
```python
import jax
import jax.numpy as jnp
from jax import lax
from jax.sharding import PartitionSpec as P

D = 2880
QUERY_HEADS = 64
KEY_VALUE_HEADS = 8
HEAD_SIZE = 64
TOP = 4
SHARED_CONTEXTS = 2


clamp_limit = 7.0


def combined_all(x, axis, combine):
    everything = jax.tree.map(
        lambda part, kind: lax.all_gather(part.astype(kind), axis),
        x,
        jax.tree.map(lambda a: jnp.bfloat16 if a.dtype == jnp.float32 else a.dtype, x),
    )

    def take(k):
        return jax.tree.map(lambda part, own: part[k].astype(own.dtype), everything, x)

    return lax.fori_loop(
        1, lax.axis_size(axis), lambda k, so_far: combine(so_far, take(k)), take(0)
    )


def merge_parts(first, second):
    first_max, first_total, first_out = first
    second_max, second_total, second_out = second
    joint_max = jnp.maximum(first_max, second_max)
    first_factor = jnp.exp(first_max - joint_max)
    second_factor = jnp.exp(second_max - joint_max)
    joint_total = first_total * first_factor + second_total * second_factor
    decode_row_count, head_count = first_max.shape
    joint_out = (
        first_out.reshape(decode_row_count, head_count, -1) * first_factor[:, :, None]
        + second_out.reshape(decode_row_count, head_count, -1) * second_factor[:, :, None]
    )
    return (joint_max, joint_total, joint_out.reshape(decode_row_count, -1))


def local_partials(grouped_heads, shared_context_cache, branch):
    decode_row_count = grouped_heads.shape[0]
    score_scale = HEAD_SIZE ** (-0.5)
    current = None
    for context_slot in range(SHARED_CONTEXTS):
        cached_key_block = shared_context_cache[
            context_slot, :, : KEY_VALUE_HEADS * HEAD_SIZE
        ].reshape(-1, KEY_VALUE_HEADS, HEAD_SIZE)
        cached_value_block = shared_context_cache[
            context_slot, :, KEY_VALUE_HEADS * HEAD_SIZE :
        ].reshape(-1, KEY_VALUE_HEADS, HEAD_SIZE)
        scores = (
            jnp.einsum(
                "rgqd,tgd->rgqt",
                grouped_heads,
                cached_key_block,
                preferred_element_type=jnp.float32,
            )
            * score_scale
        )
        local_max = jnp.max(scores, axis=-1)
        weights = jnp.exp(scores - local_max[..., None])
        local_total = jnp.sum(weights, axis=-1)
        local_out = jnp.einsum(
            "rgqt,tgd->rgqd",
            weights.astype(jnp.bfloat16),
            cached_value_block,
            preferred_element_type=jnp.float32,
        )
        if current is None:
            current = (local_max, local_total, local_out)
        else:
            chosen = branch == context_slot
            current = (
                jnp.where(chosen[:, None, None], local_max, current[0]),
                jnp.where(chosen[:, None, None], local_total, current[1]),
                jnp.where(chosen[:, None, None, None], local_out, current[2]),
            )
    return (
        current[0].reshape(decode_row_count, QUERY_HEADS),
        current[1].reshape(decode_row_count, QUERY_HEADS),
        current[2].reshape(decode_row_count, QUERY_HEADS * HEAD_SIZE),
    )


def finish_attention(merged, grouped_heads, row_key_value, sink_logits):
    decode_row_count = grouped_heads.shape[0]
    heads_per_group = QUERY_HEADS // KEY_VALUE_HEADS
    score_scale = HEAD_SIZE ** (-0.5)
    cache_max, cache_total, cache_out = merged
    row_own_keys = (
        row_key_value[:, : KEY_VALUE_HEADS * HEAD_SIZE]
        .reshape(decode_row_count, KEY_VALUE_HEADS, 1, HEAD_SIZE)
        .astype(jnp.float32)
    )
    row_own_values = (
        row_key_value[:, KEY_VALUE_HEADS * HEAD_SIZE :]
        .reshape(decode_row_count, KEY_VALUE_HEADS, 1, HEAD_SIZE)
        .astype(jnp.float32)
    )
    own_score = (
        jnp.sum(grouped_heads.astype(jnp.float32) * row_own_keys, axis=-1) * score_scale
    ).reshape(decode_row_count, QUERY_HEADS)
    row_own_values = jnp.broadcast_to(
        row_own_values, (decode_row_count, KEY_VALUE_HEADS, heads_per_group, HEAD_SIZE)
    ).reshape(decode_row_count, QUERY_HEADS, HEAD_SIZE)
    sink_row = sink_logits[None, :]
    peak = jnp.maximum(jnp.maximum(cache_max, own_score), sink_row)
    cache_factor = jnp.exp(cache_max - peak)
    own_factor = jnp.exp(own_score - peak)
    sink_factor = jnp.exp(sink_row - peak)
    denominator = cache_total * cache_factor + own_factor + sink_factor
    numerator = (
        cache_out.reshape(decode_row_count, QUERY_HEADS, HEAD_SIZE) * cache_factor[..., None]
        + own_factor[..., None] * row_own_values
    )
    return (
        (numerator / denominator[..., None])
        .reshape(decode_row_count, QUERY_HEADS * HEAD_SIZE)
        .astype(jnp.bfloat16)
    )


def shards(
    queries,
    row_key_value,
    shared_context_cache,
    branch,
    sink_logits,
    w_out,
    residual,
    norm_gain,
    expert_ids,
    weight_codes,
    w_gate,
    w_up,
    w_down,
):
    decode_row_count = queries.shape[0]
    grouped_heads = queries.reshape(
        decode_row_count, KEY_VALUE_HEADS, QUERY_HEADS // KEY_VALUE_HEADS, HEAD_SIZE
    )
    partial_stats = local_partials(grouped_heads, shared_context_cache, branch)
    merged = combined_all(partial_stats, "att", merge_parts)
    attention = finish_attention(merged, grouped_heads, row_key_value, sink_logits)
    projected = jnp.dot(attention, w_out, preferred_element_type=jnp.float32)
    hidden = residual.astype(jnp.float32) + projected
    attended = hidden.astype(jnp.bfloat16)
    squares = lax.psum(jnp.sum(hidden * hidden, axis=1), "att")
    inverse = lax.rsqrt(squares / D + 1e-05)
    normed = (hidden * inverse[:, None] * norm_gain.astype(jnp.float32)[None, :]).astype(
        jnp.bfloat16
    )
    local_experts = w_gate.shape[0]
    expert_count = local_experts * lax.axis_size("exp")
    capacity = min(decode_row_count, max(2, 2 * decode_row_count * TOP // expert_count))
    flat_ids = expert_ids.reshape(-1)
    expert_hits = (flat_ids[:, None] == jnp.arange(expert_count, dtype=jnp.int32)[None, :]).astype(
        jnp.int32
    )
    earlier = jnp.cumsum(expert_hits, axis=0) - expert_hits
    position = jnp.sum(earlier * expert_hits, axis=1)
    slot_index = flat_ids * capacity + position
    placed = slot_index[None, :] == jnp.arange(expert_count * capacity, dtype=jnp.int32)[:, None]
    assign = jnp.any(placed.reshape(expert_count * capacity, decode_row_count, TOP), axis=2).astype(
        jnp.bfloat16
    )
    source_rows = lax.all_gather(normed, "att", axis=1, tiled=True)
    outgoing = jnp.dot(assign, source_rows, preferred_element_type=jnp.float32).astype(jnp.bfloat16)
    outgoing = outgoing.reshape(expert_count, capacity, -1)
    received = lax.all_to_all(outgoing, "exp", split_axis=0, concat_axis=0, tiled=True)
    senders = received.shape[0] // local_experts
    slot_count = received.shape[1]
    arranged = received.reshape(senders, local_experts, slot_count, received.shape[2])
    gate_sum = jnp.einsum("sekd,edf->sekf", arranged, w_gate, preferred_element_type=jnp.float32)
    up_sum = jnp.einsum("sekd,edf->sekf", arranged, w_up, preferred_element_type=jnp.float32)
    gate_sum = jnp.minimum(gate_sum, clamp_limit)
    up_sum = jnp.clip(up_sum, -clamp_limit, clamp_limit)
    active = (gate_sum * jax.nn.sigmoid(1.702 * gate_sum) * (up_sum + 1.0)).astype(jnp.bfloat16)
    partial_out = jnp.einsum("sekf,efd->sekd", active, w_down, preferred_element_type=jnp.float32)
    summed = lax.psum_scatter(
        partial_out.astype(jnp.bfloat16), "att", scatter_dimension=3, tiled=True
    )
    answer = lax.all_to_all(
        summed.reshape(senders * local_experts, slot_count, -1),
        "exp",
        split_axis=0,
        concat_axis=0,
        tiled=True,
    )
    flat_returned = answer.reshape(expert_count * capacity, -1)
    picked = flat_returned[slot_index].reshape(decode_row_count, TOP, -1).astype(jnp.float32)
    shares = weight_codes.astype(jnp.float32)
    shares = shares / jnp.sum(shares, axis=1, keepdims=True)
    mixture = jnp.sum(picked * shares[:, :, None], axis=1).astype(jnp.bfloat16)
    return (attended, mixture)


def solution(mesh):
    placed = (
        P(("groups", "exp"), None),
        P(("groups", "exp"), None),
        P("groups", "att", None),
        P(("groups", "exp")),
        P(),
        P(None, "att"),
        P(("groups", "exp"), "att"),
        P("att"),
        P(("groups", "exp"), None),
        P(("groups", "exp"), None),
        P("exp", None, "att"),
        P("exp", None, "att"),
        P("exp", "att", None),
    )
    return jax.shard_map(
        shards,
        mesh=mesh,
        in_specs=placed,
        out_specs=(P(("groups", "exp"), "att"), P(("groups", "exp"), "att")),
        check_vma=False,
    )
```

profile of v0, /device:TPU:0, one launch (start us, length us, event | category | flops | bytes accessed | tf_op | source)
XLA Modules:
  0.0 310.6 jit_solution(5076285641366999604)
XLA Ops:
  7.2 2.6 fusion.91
  12.4 4.5 %bitcast_reduce_fusion = (f32[64,8,8]{0,2,1:T(8,128)S(1)}, f32[8,512,64,8]{1,2,3,0:T(8,128)}) fusion(bf16[512,8,64,1]{0,2,3,1:T(8,128)(2,1)S(1)} %bitcast.226, bf16[64,8,8,64]{3,2,1,0:T(8,128)(2,1)S(1)} %reshape.381), kind=kOutput, calls=%fused_computation.8 | convolution fusion | flops 272625664 | bytes 9453568 | tf_op jit(solution)/shard_map/rgqd,tgd->rgqt/dot_general | solution.py:59
  16.9 4.5 %bitcast_reduce_fusion.1 = (f32[64,8,8]{0,2,1:T(8,128)S(1)}, f32[8,512,64,8]{1,2,3,0:T(8,128)}) fusion(bf16[512,8,64,1]{0,2,3,1:T(8,128)(2,1)S(1)} %bitcast.225, bf16[64,8,8,64]{3,2,1,0:T(8,128)(2,1)S(1)} %reshape.381), kind=kOutput, calls=%fused_computation.11 | convolution fusion | flops 272625664 | bytes 9453568 | tf_op jit(solution)/shard_map/rgqd,tgd->rgqt/dot_general | solution.py:59
  21.9 8.0 %fusion.9 = (bf16[64,8,8,512]{3,0,2,1:T(8,128)(2,1)S(1)}, bf16[64,8,8]{0,2,1:T(8,128)(2,1)S(1)}, bf16[64,8,8]{0,2,1:T(8,128)(2,1)S(1)}, bf16[64,8,8,512]{3,0,2,1:T(8,128)(2,1)S(1)}) fusion(f32[8,512,64,8]{1,2,3,0:T(8,128)} %get-tuple-element.57, f32[64,8,8]{0,2,1:T(8,128)S(1)} %get-tuple-element.56, f32[64,8,8]{0,2,1:T(8,128)S(1)} %get-tuple-element.54, ...), kind=kLoop, calls=%fused_computation.14 | loop fusion | flops 16769024 | bytes 25214976 | tf_op jit(solution)/shard_map/convert_element_type | solution.py:72
  29.9 2.4 fusion.15
  32.3 2.6 fusion.55
  37.1 5.4 %all_gather.16 = bf16[2,64,64]{2,1,0:T(8,128)(2,1)S(1)} all-gather(bf16[1,64,64]{2,1,0:T(8,128)(2,1)S(1)} %copy.132), channel_id=1, replica_groups=mesh['groups'=2,'att'=2,'exp'=8] {'att'}, dimensions={0}, use_global_device_ids=true | all-gather | bytes 24576 | tf_op jit(solution)/shard_map/all_gather | solution.py:19
  42.5 4.6 %all_gather.17 = bf16[2,64,64]{2,1,0:T(8,128)(2,1)S(1)} all-gather(bf16[1,64,64]{2,1,0:T(8,128)(2,1)S(1)} %copy.140), channel_id=1, replica_groups=mesh['groups'=2,'att'=2,'exp'=8] {'att'}, dimensions={0}, use_global_device_ids=true | all-gather | bytes 24576 | tf_op jit(solution)/shard_map/all_gather | solution.py:19
  57.9 1.7 mul.198
  63.7 9.9 %multiply_reduce_fusion.2 = (f32[64]{0:T(128)S(1)}, f32[64,1440]{1,0:T(8,128)S(1)}) fusion(bf16[4096,1440]{0,1:T(8,128)(2,1)} %param.18, f32[64,4096]{1,0:T(8,128)S(1)} %div.29, f32[64,4096]{1,0:T(8,128)} %mul.198, f32[64,4096]{1,0:T(8,128)} %reshape.382, f32[64,4096]{1,0:T(8,128)} %mul.195, f32[64,4096]{1,0:T(8,128)} %mul.187, f32[64,4096]{1,0:T(8,128)} %mul.184, ...), kind=kOutput, calls=%fused_computation.58 | convolution fusion | flops 757964736 | bytes 19689728 | tf_op jit(solution)/shard_map/dot_general | solution.py:152
  73.6 4.9 %psum.7 = f32[64]{0:T(128)S(1)} all-reduce(f32[64]{0:T(128)S(1)} %get-tuple-element.58), channel_id=1, replica_groups=mesh['groups'=2,'att'=2,'exp'=8] {'att'}, use_global_device_ids=true, to_apply=%region_10.11 | all-reduce | flops 64 | bytes 512 | tf_op jit(solution)/shard_map/psum | solution.py:155
  79.3 6.3 %all-gather = bf16[2,1440,64]{1,2,0:T(8,128)(2,1)S(1)} all-gather(bf16[1,1440,64]{1,2,0:T(8,128)(2,1)S(1)} %get-tuple-element.34), channel_id=1, replica_groups=mesh['groups'=2,'att'=2,'exp'=8] {'att'}, dimensions={0}, use_global_device_ids=true | all-gather | bytes 552960 | tf_op jit(solution)/shard_map/all_gather | solution.py:174
  87.3 3.0 copy.149
  90.3 74.1 %all_to_all.10 = bf16[8,64,2880]{2,1,0:T(8,128)(2,1)S(1)} all-to-all(bf16[8,64,2880]{2,1,0:T(8,128)(2,1)} %bitcast.222), channel_id=1, replica_groups=mesh['groups'=2,'att'=2,'exp'=8] {'exp'}, dimensions={0} | all-to-all | bytes 5898240 | tf_op jit(solution)/shard_map/all_to_all | solution.py:177
  164.4 10.1 %fusion.28 = f32[8,1,64,1440]{3,2,0,1:T(8,128)} fusion(bf16[8,64,2880]{2,1,0:T(8,128)(2,1)S(1)} %all_to_all.10, bf16[1,2880,1440]{1,2,0:T(8,128)(2,1)} %param.23), kind=kOutput, calls=%fused_computation.26 | convolution fusion | flops 4247470080 | bytes 14192640 | tf_op jit(solution)/shard_map/sekd,edf->sekf/dot_general | solution.py:181
  174.5 18.8 %fusion.19 = bf16[8,1,64,2880]{3,2,0,1:T(8,128)(2,1)} fusion(bf16[1,1440,2880]{2,1,0:T(8,128)(2,1)} %param.25, bf16[8,64,2880]{2,1,0:T(8,128)(2,1)S(1)} %all_to_all.10, bf16[1,2880,1440]{1,2,0:T(8,128)(2,1)} %param.24, f32[8,1,64,1440]{3,2,0,1:T(8,128)} %fusion.28), kind=kOutput, calls=%fused_computation.23 | convolution fusion | flops 8501575680 | bytes 25436160 | tf_op jit(solution)/shard_map/sekf,efd->sekd/dot_general | solution.py:186
  193.3 7.7 %copy.155 = bf16[8,1,64,2880]{2,0,1,3:T(8,128)(2,1)} copy(bf16[8,1,64,2880]{3,2,0,1:T(8,128)(2,1)} %fusion.19) | data formatting | bytes 5898240
  201.0 8.9 %reshape.417 = bf16[2880,512]{1,0:T(8,128)(2,1)} reshape(bf16[2880,1,8,64]{3,2,1,0:T(8,128)(2,1)} %bitcast.221) | data formatting | bytes 5898240
  209.9 40.4 %reduce-scatter.4.cloned.1.call-done = bf16[1440,512]{1,0:T(8,128)(2,1)} async-done(((bf16[2880,512]{1,0:T(8,128)(2,1)}), bf16[1440,512]{1,0:T(8,128)(2,1)}) %reduce-scatter.4.cloned.1.call-update) | async-done | bytes 1474576
  250.3 3.8 %reshape.418 = bf16[1440,1,8,64]{3,2,1,0:T(8,128)(2,1)S(1)} reshape(bf16[1440,512]{1,0:T(8,128)(2,1)} %reduce-scatter.4.cloned.1.call-done) | data formatting | bytes 2949120
  254.1 3.6 %copy.156 = bf16[8,1,64,1440]{3,2,0,1:T(8,128)(2,1)} copy(bf16[8,1,64,1440]{2,0,1,3:T(8,128)(2,1)S(1)} %bitcast.223) | data formatting | bytes 2949120
  257.7 4.6 %all-to-all-start.1 = ((bf16[8,64,1440]{2,1,0:T(8,128)(2,1)}), bf16[8,64,1440]{2,1,0:T(8,128)(2,1)S(1)}, u32[]{:S(2)}, u32[]{:S(2)}) async-start(bf16[8,64,1440]{2,1,0:T(8,128)(2,1)} %bitcast.224), calls=%async_computation.1 | async-start | bytes 3145728 | tf_op jit(solution)/shard_map/all_to_all | solution.py:190
  262.5 37.5 %all-to-all-done.1 = bf16[8,64,1440]{2,1,0:T(8,128)(2,1)S(1)} async-done(((bf16[8,64,1440]{2,1,0:T(8,128)(2,1)}), bf16[8,64,1440]{2,1,0:T(8,128)(2,1)S(1)}, u32[]{:S(2)}, u32[]{:S(2)}) %all-to-all-start.1) | async-done | bytes 1474592 | tf_op jit(solution)/shard_map/all_to_all | solution.py:190
  301.9 1.8 multiply_reduce_fusion.1
  (87 shorter events, 24.4 us)
Async XLA Ops:
  7.2 2.8 copy-start
  7.2 56.6 %all-gather.3.cloned.1.call-start = ((), (), s32[]{:S(2)}) async-start(), calls=%async_computation.3 | async-start | bytes 1572864 | tf_op jit(solution)/shard_map/all_gather | solution.py:19
  16.9 4.5 %copy-start.7 = (s32[64]{0:T(128)S(1)}, s32[64]{0:T(128)}, u32[]{:S(2)}) copy-start(s32[64]{0:T(128)} %param.16) | copy-start | bytes 772
  34.9 12.2 %copy-start.2 = (bf16[64,1024]{1,0:T(8,128)(2,1)S(1)}, bf16[64,1024]{1,0:T(8,128)(2,1)}, u32[]{:S(2)}) copy-start(bf16[64,1024]{1,0:T(8,128)(2,1)} %param.14) | copy-start | bytes 393220
  34.9 13.0 %copy-start.5 = (s32[64,4]{0,1:T(4,128)S(1)}, s32[64,4]{0,1:T(4,128)}, u32[]{:S(2)}) copy-start(s32[64,4]{0,1:T(4,128)} %param.21) | copy-start | bytes 3076
  35.2 13.5 %copy-start.6 = (f32[64]{0:T(128)S(1)}, f32[64]{0:T(128)}, u32[]{:S(2)}) copy-start(f32[64]{0:T(128)} %param.17) | copy-start | bytes 772
  36.9 213.4 %reduce-scatter.4.cloned.1.call-start = ((), (), s32[]{:S(2)}) async-start(), calls=%async_computation.4 | async-start | bytes 4423680
  48.0 0.9 copy-start.1
  59.6 2.0 copy-start.4
  254.1 8.3 %copy-start.3 = (s32[64,4]{0,1:T(4,128)S(1)}, s32[64,4]{0,1:T(4,128)}, u32[]{:S(2)}) copy-start(s32[64,4]{0,1:T(4,128)} %param.22) | copy-start | bytes 3076
  257.7 42.4 %all-to-all-start.1 = ((bf16[8,64,1440]{2,1,0:T(8,128)(2,1)}), bf16[8,64,1440]{2,1,0:T(8,128)(2,1)S(1)}, u32[]{:S(2)}, u32[]{:S(2)}) async-start(bf16[8,64,1440]{2,1,0:T(8,128)(2,1)} %bitcast.224), calls=%async_computation.1 | async-start | bytes 3145728 | tf_op jit(solution)/shard_map/all_to_all | solution.py:190
Sparse Core Ops, SparseCore 0:
  37.0 23.9 all-gather.2
  210.0 40.1 reduce-scatter.3
where the time goes:
time: 316 us; the launch traced here: 311 us
  blocking collectives  95.3 us (30%)
  waiting for transfers between devices  78 us (25%)
  matrix products  53.9 us (17%)
  local copies, waits for them, and re-layouts  51.3 us (16%)
  between operations  14.5 us (5%)
  other arithmetic  12.9 us (4%)
  starting transfers between devices  4.7 us (1%)
    all_to_all x1, blocking collectives, shards(): lax.all_to_all(outgoing, 'exp', split_axis=0, concat_axis=0, tiled=True)  74.1 us
    unnamed x3, waiting for transfers between devices  40.4 us
    all_to_all x1, waiting for transfers between devices, shards(): lax.all_to_all(summed.reshape(senders * local_experts, slot_count, -1), '...  37.5 us
    unnamed x26, local copies, waits for them, and re-layouts  24.7 us
    dot_general x1, matrix products, shards(): jnp.einsum('sekf,efd->sekd', active, w_down, preferred_element_type=jnp.f...  18.8 us
    dot_general x1, matrix products, shards(): jnp.einsum('sekd,edf->sekf', arranged, w_gate, preferred_element_type=jnp...  10.1 us
    all_gather x2, blocking collectives, combined_all(): lax.all_gather(part.astype(kind), axis)  9.97 us
    dot_general x1, matrix products, shards(): projected = jnp.dot(attention, w_out, preferred_element_type=jnp.float32)  9.88 us
  transfers between devices with their start and end apart: 3, of which 2 were waited for; matrix products, arithmetic and copies ran while one was open for 5% of the time, Pallas kernels for 0%

commit v1 on v0

--- a/solution.py
+++ b/solution.py
@@ -1,6 +1,10 @@
+import functools
+
 import jax
 import jax.numpy as jnp
 from jax import lax
+from jax.experimental import pallas as pl
+from jax.experimental.pallas import tpu as pltpu
 from jax.sharding import PartitionSpec as P
 
 D = 2880
@@ -11,6 +15,7 @@
 SHARED_CONTEXTS = 2
 
 
+MESH = pl.DeviceIdType.MESH
 clamp_limit = 7.0
 
 
@@ -126,6 +131,457 @@
         .astype(jnp.bfloat16)
     )
 
+def moe_kernel(
+    n,
+    u_ref,
+    meta_ref,
+    wg_hbm,
+    wu_hbm,
+    wd_hbm,
+    out_ref,
+    wg,
+    wu,
+    wd,
+    X,
+    META,
+    act_ref,
+    P_ref,
+    CS,
+    SR,
+    SL,
+    RR,
+    RL,
+    YS,
+    YR,
+    wsem,
+    xsend,
+    xrecv,
+    msend,
+    mrecv,
+    csend,
+    crecv,
+    rsend,
+    rrecv,
+    ysend,
+    yrecv,
+):
+    rings = n // 2
+    half_ring = rings // 2
+    rows = u_ref.shape[0]
+    width = u_ref.shape[1]
+    half_rows = rows // 2
+    experts = meta_ref.shape[0]
+    a = lax.axis_index("att")
+    e = lax.axis_index("exp")
+    z = e // 2
+    c = e % 2
+
+    def at(offset):
+        return lax.rem(z + offset + rings, rings)
+
+    def lane(offset):
+        return at(offset) * 2 + c
+
+    right = {"exp": lane(1)}
+    left = {"exp": lane(-1)}
+    mate = {"exp": z * 2 + 1 - c}
+    across = {"att": 1 - a}
+
+    loads = [
+        pltpu.make_async_copy(wg_hbm.at[0], wg, wsem.at[0]),
+        pltpu.make_async_copy(wu_hbm.at[0], wu, wsem.at[1]),
+        pltpu.make_async_copy(wd_hbm.at[0], wd, wsem.at[2]),
+    ]
+    for load in loads:
+        load.start()
+
+    barrier = pltpu.get_barrier_semaphore()
+    for target in (right, left, mate, across):
+        pl.semaphore_signal(barrier, inc=1, device_id=target, device_id_type=MESH)
+    pl.semaphore_wait(barrier, 4)
+
+    pending = []
+    counter = [0]
+
+    def send(src_x, src_m, h, idx, target, part=None):
+        k = counter[0]
+        counter[0] += 1
+        if part is None:
+            dst_x, slot = X.at[h, idx], 0
+        else:
+            dst_x, slot = X.at[h, idx, pl.ds(part * half_rows, half_rows)], part
+        x_copy = pltpu.make_async_remote_copy(
+            src_ref=src_x,
+            dst_ref=dst_x,
+            send_sem=xsend.at[k],
+            recv_sem=xrecv.at[h, idx, slot],
+            device_id=target,
+            device_id_type=MESH,
+        )
+        x_copy.start()
+        pending.append(x_copy)
+        if part is None or part == 0:
+            m_copy = pltpu.make_async_remote_copy(
+                src_ref=src_m,
+                dst_ref=META.at[h, idx],
+                send_sem=msend.at[k],
+                recv_sem=mrecv.at[h, idx],
+                device_id=target,
+                device_id_type=MESH,
+            )
+            m_copy.start()
+            pending.append(m_copy)
+
+    def arrived(h, idx, part=None):
+        if part is None:
+            ref, slot = X.at[h, idx], 0
+        else:
+            ref, slot = X.at[h, idx, pl.ds(part * half_rows, half_rows)], part
+        pltpu.make_async_remote_copy(
+            src_ref=ref,
+            dst_ref=ref,
+            send_sem=xsend.at[0],
+            recv_sem=xrecv.at[h, idx, slot],
+            device_id=mate,
+            device_id_type=MESH,
+        ).wait_recv()
+        if part is None or part == 0:
+            pltpu.make_async_remote_copy(
+                src_ref=META.at[h, idx],
+                dst_ref=META.at[h, idx],
+                send_sem=msend.at[0],
+                recv_sem=mrecv.at[h, idx],
+                device_id=mate,
+                device_id_type=MESH,
+            ).wait_recv()
+
+    halves = (a, 1 - a)
+    send(u_ref, meta_ref, a, e, across)
+    send(u_ref, meta_ref, a, e, right)
+    send(u_ref, meta_ref, a, e, left)
+    send(u_ref, meta_ref, a, e, mate)
+    X[a, e] = u_ref[...]
+    META[a, e] = meta_ref[...]
+    arrived(1 - a, e)
+    own = (1 - a, e)
+    for target in (right, left, mate):
+        send(X.at[own], META.at[own], 1 - a, e, target)
+
+    def forward(step, h):
+        from_left, from_right = lane(-step), lane(step)
+        if step < half_ring:
+            last = step + 1 == half_ring
+            arrived(h, from_left)
+            if last:
+                lo = pl.ds(0, half_rows)
+                send(X.at[h, from_left, lo], META.at[h, from_left], h, from_left, right, 0)
+            else:
+                send(X.at[h, from_left], META.at[h, from_left], h, from_left, right)
+            arrived(h, from_right)
+            if last:
+                hi = pl.ds(half_rows, half_rows)
+                send(X.at[h, from_right, hi], None, h, from_right, left, 1)
+            else:
+                send(X.at[h, from_right], META.at[h, from_right], h, from_right, left)
+            send(X.at[h, from_left], META.at[h, from_left], h, from_left, mate)
+            send(X.at[h, from_right], META.at[h, from_right], h, from_right, mate)
+        else:
+            arrived(h, from_left, 0)
+            arrived(h, from_left, 1)
+            send(X.at[h, from_left], META.at[h, from_left], h, from_left, mate)
+
+    def mates(step, h):
+        arrived(h, at(-step) * 2 + 1 - c)
+        if 0 < step < half_ring:
+            arrived(h, at(step) * 2 + 1 - c)
+
+    eye = lax.broadcasted_iota(jnp.int32, (rows, rows), 0) == lax.broadcasted_iota(
+        jnp.int32, (rows, rows), 1
+    )
+
+    def upright(row):
+        return jnp.sum(jnp.where(eye, jnp.broadcast_to(row, (rows, rows)), 0.0), axis=1, keepdims=True)
+
+    def run_chunk(offsets):
+        blocks = [at(o) * 2 + k for o in offsets for k in range(2)]
+        count = len(blocks) * rows
+        x0 = jnp.concatenate([X[0, b] for b in blocks], axis=0)
+        x1 = jnp.concatenate([X[1, b] for b in blocks], axis=0)
+        shares, inverses = [], []
+        pick = lax.broadcasted_iota(jnp.int32, (experts, 2 * rows), 0) == e
+        for b in blocks:
+            squares = META[0, b][0:1, rows : 2 * rows] + META[1, b][0:1, rows : 2 * rows]
+            inverses.append(upright(lax.rsqrt(squares / (2 * width) + 1e-05)))
+            mine = jnp.sum(jnp.where(pick, META[0, b], 0.0), axis=0, keepdims=True)
+            shares.append(upright(mine[:, :rows]))
+        inverse = jnp.concatenate(inverses, axis=0)
+        share = jnp.concatenate(shares, axis=0)
+
+        def first(start, size):
+            cols = pl.ds(start, size)
+            g = jnp.dot(x0, wg[:width, cols], preferred_element_type=jnp.float32)
+            g += jnp.dot(x1, wg[width:, cols], preferred_element_type=jnp.float32)
+            u = jnp.dot(x0, wu[:width, cols], preferred_element_type=jnp.float32)
+            u += jnp.dot(x1, wu[width:, cols], preferred_element_type=jnp.float32)
+            g = jnp.minimum(g * inverse, clamp_limit)
+            u = jnp.clip(u * inverse, -clamp_limit, clamp_limit)
+            act_ref[:, cols] = (g * jax.nn.sigmoid(1.702 * g) * (u + 1.0)).astype(jnp.bfloat16)
+
+        def second(start, size):
+            cols = pl.ds(start, size)
+            y = jnp.dot(act_ref[...], wd[:, cols], preferred_element_type=jnp.float32)
+            y = (y * share).astype(jnp.bfloat16)
+            for k, b in enumerate(blocks):
+                P_ref[b, :, cols] = y[k * rows : (k + 1) * rows]
+
+        def tiled(body, total, tile):
+            whole_tiles = total // tile
+
+            @pl.loop(0, whole_tiles)
+            def _(i):
+                body(pl.multiple_of(i * tile, tile), tile)
+
+            if total % tile:
+                body(whole_tiles * tile, total % tile)
+
+        return tiled, first, second
+
+    order = [0]
+    for s in range(1, half_ring):
+        order += [-s, s]
+    order += [half_ring]
+    chunks = [order[k : k + 2] for k in range(0, len(order), 2)]
+
+    c_copies = []
+
+    def swap(offset):
+        dest = at(offset)
+        k = offset % rings
+        copy = pltpu.make_async_remote_copy(
+            src_ref=P_ref.at[dest * 2 + 1 - c],
+            dst_ref=CS.at[dest],
+            send_sem=csend.at[k],
+            recv_sem=crecv.at[dest],
+            device_id=mate,
+            device_id_type=MESH,
+        )
+        copy.start()
+        return copy
+
+    for step in range(1, half_ring + 1):
+        for h in halves:
+            forward(step, h)
+    for step in range(0, half_ring + 1):
+        for h in halves:
+            mates(step, h)
+    loads[0].wait()
+    loads[1].wait()
+    loads[2].wait()
+    swaps = {}
+    for offsets in chunks[::-1]:
+        tiled, first, second = run_chunk(offsets)
+        tiled(first, width, 256)
+        tiled(second, 2 * width, 256)
+        for o in offsets:
+            swaps[o % rings] = swap(o)
+
+    def chip_sum(offset):
+        dest = at(offset)
+        return P_ref[dest * 2 + c].astype(jnp.float32) + CS[dest].astype(jnp.float32)
+
+    ring_copies = []
+
+    def ring_copy(src, dst, k, d, target):
+        copy = pltpu.make_async_remote_copy(
+            src_ref=src,
+            dst_ref=dst,
+            send_sem=rsend.at[k, d - 1],
+            recv_sem=rrecv.at[k, d - 1],
+            device_id=target,
+            device_id_type=MESH,
+        )
+        copy.start()
+        ring_copies.append(copy)
+        return copy
+
+    coming = {}
+    lo = pl.ds(0, half_rows)
+    hi = pl.ds(half_rows, half_rows)
+    swapped = set()
+
+    def swap_done(offset):
+        k = offset % rings
+        if k not in swapped:
+            swapped.add(k)
+            swaps[k].wait()
+
+    for d in range(half_ring, 0, -1):
+        swap_done(d)
+        swap_done(-d)
+        if d == half_ring:
+            total = chip_sum(d).astype(jnp.bfloat16)
+            SR[d - 1, lo] = total[:half_rows]
+            SL[d - 1, hi] = total[half_rows:]
+            coming[0] = ring_copy(SR.at[d - 1, lo], RR.at[d - 1, lo], 0, d, right)
+            coming[1] = ring_copy(SL.at[d - 1, hi], RL.at[d - 1, hi], 1, d, left)
+            continue
+        if d + 1 == half_ring:
+            to_right = chip_sum(d)
+            to_left = chip_sum(-d)
+            coming[0].wait_recv()
+            SR[d - 1, lo] = (to_right[:half_rows] + RR[d, lo].astype(jnp.float32)).astype(jnp.bfloat16)
+            SR[d - 1, hi] = to_right[half_rows:].astype(jnp.bfloat16)
+            coming[0] = ring_copy(SR.at[d - 1], RR.at[d - 1], 0, d, right)
+            coming[1].wait_recv()
+            SL[d - 1, hi] = (to_left[half_rows:] + RL[d, hi].astype(jnp.float32)).astype(jnp.bfloat16)
+            SL[d - 1, lo] = to_left[:half_rows].astype(jnp.bfloat16)
+            coming[1] = ring_copy(SL.at[d - 1], RL.at[d - 1], 1, d, left)
+        else:
+            coming[0].wait_recv()
+            SR[d - 1] = (chip_sum(d) + RR[d].astype(jnp.float32)).astype(jnp.bfloat16)
+            coming[0] = ring_copy(SR.at[d - 1], RR.at[d - 1], 0, d, right)
+            coming[1].wait_recv()
+            SL[d - 1] = (chip_sum(-d) + RL[d].astype(jnp.float32)).astype(jnp.bfloat16)
+            coming[1] = ring_copy(SL.at[d - 1], RL.at[d - 1], 1, d, left)
+    swap_done(0)
+    total = chip_sum(0)
+    coming[0].wait_recv()
+    coming[1].wait_recv()
+    total = total + RR[0].astype(jnp.float32) + RL[0].astype(jnp.float32)
+    low, high = total[:, :width], total[:, width:]
+    mine = jnp.where(a == 0, low, high)
+    YS[...] = jnp.where(a == 0, high, low).astype(jnp.bfloat16)
+    last = pltpu.make_async_remote_copy(
+        src_ref=YS,
+        dst_ref=YR,
+        send_sem=ysend,
+        recv_sem=yrecv,
+        device_id=across,
+        device_id_type=MESH,
+    )
+    last.start()
+    for copy in pending + ring_copies:
+        copy.wait_send()
+    last.wait()
+    out_ref[...] = (mine + YR[...].astype(jnp.float32)).astype(jnp.bfloat16)
+
+
+def moe(u, meta, w_gate, w_up, w_down):
+    n = lax.axis_size("exp")
+    rings = n // 2
+    half_ring = max(1, rings // 2)
+    rows, width = u.shape
+    full = 2 * width
+    experts = meta.shape[0]
+    per_chunk = 4 * rows
+    sends = 4 * n + 8
+    bf = jnp.bfloat16
+    dma = pltpu.SemaphoreType.DMA
+    return pl.pallas_call(
+        functools.partial(moe_kernel, n),
+        out_shape=jax.ShapeDtypeStruct((rows, width), bf),
+        in_specs=[pl.BlockSpec(memory_space=pltpu.VMEM)] * 2
+        + [pl.BlockSpec(memory_space=pl.ANY)] * 3,
+        out_specs=pl.BlockSpec(memory_space=pltpu.VMEM),
+        scratch_shapes=[
+            pltpu.VMEM((full, width), bf),
+            pltpu.VMEM((full, width), bf),
+            pltpu.VMEM((width, full), bf),
+            pltpu.VMEM((2, n, rows, width), bf),
+            pltpu.VMEM((2, n, experts, 2 * rows), jnp.float32),
+            pltpu.VMEM((per_chunk, width), bf),
+            pltpu.VMEM((n, rows, full), bf),
+            pltpu.VMEM((rings, rows, full), bf),
+            pltpu.VMEM((half_ring, rows, full), bf),
+            pltpu.VMEM((half_ring, rows, full), bf),
+            pltpu.VMEM((half_ring, rows, full), bf),
+            pltpu.VMEM((half_ring, rows, full), bf),
+            pltpu.VMEM((rows, width), bf),
+            pltpu.VMEM((rows, width), bf),
+            dma((3,)),
+            dma((sends,)),
+            dma((2, n, 2)),
+            dma((sends,)),
+            dma((2, n)),
+            dma((rings,)),
+            dma((rings,)),
+            dma((2, half_ring)),
+            dma((2, half_ring)),
+            dma,
+            dma,
+        ],
+        compiler_params=pltpu.CompilerParams(
+            collective_id=1, has_side_effects=True, vmem_limit_bytes=62 * 1024 * 1024
+        ),
+    )(u, meta, w_gate, w_up, w_down)
+
+
+def ringed_experts(hidden, norm_gain, expert_ids, weight_codes, w_gate, w_up, w_down):
+    rows = hidden.shape[0]
+    squares = jnp.sum(hidden * hidden, axis=1)
+    scaled = (hidden * norm_gain.astype(jnp.float32)[None, :]).astype(jnp.bfloat16)
+    expert_count = w_gate.shape[0] * lax.axis_size("exp")
+    shares = weight_codes.astype(jnp.float32)
+    shares = shares / jnp.sum(shares, axis=1, keepdims=True)
+    named = expert_ids[None, :, :] == jnp.arange(expert_count, dtype=jnp.int32)[:, None, None]
+    by_expert = jnp.sum(jnp.where(named, shares[None], 0.0), axis=2)
+    meta = jnp.concatenate(
+        [by_expert, jnp.broadcast_to(squares[None, :], (expert_count, rows))], axis=1
+    )
+    return moe(scaled, meta, w_gate, w_up, w_down)
+
+
+def routed_experts(hidden, norm_gain, expert_ids, weight_codes, w_gate, w_up, w_down):
+    decode_row_count = hidden.shape[0]
+    squares = lax.psum(jnp.sum(hidden * hidden, axis=1), "att")
+    inverse = lax.rsqrt(squares / D + 1e-05)
+    normed = (hidden * inverse[:, None] * norm_gain.astype(jnp.float32)[None, :]).astype(
+        jnp.bfloat16
+    )
+    local_experts = w_gate.shape[0]
+    expert_count = local_experts * lax.axis_size("exp")
+    capacity = min(decode_row_count, max(2, 2 * decode_row_count * TOP // expert_count))
+    flat_ids = expert_ids.reshape(-1)
+    expert_hits = (flat_ids[:, None] == jnp.arange(expert_count, dtype=jnp.int32)[None, :]).astype(
+        jnp.int32
+    )
+    earlier = jnp.cumsum(expert_hits, axis=0) - expert_hits
+    position = jnp.sum(earlier * expert_hits, axis=1)
+    slot_index = flat_ids * capacity + position
+    placed = slot_index[None, :] == jnp.arange(expert_count * capacity, dtype=jnp.int32)[:, None]
+    assign = jnp.any(placed.reshape(expert_count * capacity, decode_row_count, TOP), axis=2).astype(
+        jnp.bfloat16
+    )
+    source_rows = lax.all_gather(normed, "att", axis=1, tiled=True)
+    outgoing = jnp.dot(assign, source_rows, preferred_element_type=jnp.float32).astype(jnp.bfloat16)
+    outgoing = outgoing.reshape(expert_count, capacity, -1)
+    received = lax.all_to_all(outgoing, "exp", split_axis=0, concat_axis=0, tiled=True)
+    senders = received.shape[0] // local_experts
+    slot_count = received.shape[1]
+    arranged = received.reshape(senders, local_experts, slot_count, received.shape[2])
+    gate_sum = jnp.einsum("sekd,edf->sekf", arranged, w_gate, preferred_element_type=jnp.float32)
+    up_sum = jnp.einsum("sekd,edf->sekf", arranged, w_up, preferred_element_type=jnp.float32)
+    gate_sum = jnp.minimum(gate_sum, clamp_limit)
+    up_sum = jnp.clip(up_sum, -clamp_limit, clamp_limit)
+    active = (gate_sum * jax.nn.sigmoid(1.702 * gate_sum) * (up_sum + 1.0)).astype(jnp.bfloat16)
+    partial_out = jnp.einsum("sekf,efd->sekd", active, w_down, preferred_element_type=jnp.float32)
+    summed = lax.psum_scatter(
+        partial_out.astype(jnp.bfloat16), "att", scatter_dimension=3, tiled=True
+    )
+    answer = lax.all_to_all(
+        summed.reshape(senders * local_experts, slot_count, -1),
+        "exp",
+        split_axis=0,
+        concat_axis=0,
+        tiled=True,
+    )
+    flat_returned = answer.reshape(expert_count * capacity, -1)
+    picked = flat_returned[slot_index].reshape(decode_row_count, TOP, -1).astype(jnp.float32)
+    shares = weight_codes.astype(jnp.float32)
+    shares = shares / jnp.sum(shares, axis=1, keepdims=True)
+    mixture = jnp.sum(picked * shares[:, :, None], axis=1).astype(jnp.bfloat16)
+    return mixture
+
 
 def shards(
     queries,
@@ -152,53 +608,9 @@
     projected = jnp.dot(attention, w_out, preferred_element_type=jnp.float32)
     hidden = residual.astype(jnp.float32) + projected
     attended = hidden.astype(jnp.bfloat16)
-    squares = lax.psum(jnp.sum(hidden * hidden, axis=1), "att")
-    inverse = lax.rsqrt(squares / D + 1e-05)
-    normed = (hidden * inverse[:, None] * norm_gain.astype(jnp.float32)[None, :]).astype(
-        jnp.bfloat16
-    )
-    local_experts = w_gate.shape[0]
-    expert_count = local_experts * lax.axis_size("exp")
-    capacity = min(decode_row_count, max(2, 2 * decode_row_count * TOP // expert_count))
-    flat_ids = expert_ids.reshape(-1)
-    expert_hits = (flat_ids[:, None] == jnp.arange(expert_count, dtype=jnp.int32)[None, :]).astype(
-        jnp.int32
-    )
-    earlier = jnp.cumsum(expert_hits, axis=0) - expert_hits
-    position = jnp.sum(earlier * expert_hits, axis=1)
-    slot_index = flat_ids * capacity + position
-    placed = slot_index[None, :] == jnp.arange(expert_count * capacity, dtype=jnp.int32)[:, None]
-    assign = jnp.any(placed.reshape(expert_count * capacity, decode_row_count, TOP), axis=2).astype(
-        jnp.bfloat16
-    )
-    source_rows = lax.all_gather(normed, "att", axis=1, tiled=True)
-    outgoing = jnp.dot(assign, source_rows, preferred_element_type=jnp.float32).astype(jnp.bfloat16)
-    outgoing = outgoing.reshape(expert_count, capacity, -1)
-    received = lax.all_to_all(outgoing, "exp", split_axis=0, concat_axis=0, tiled=True)
-    senders = received.shape[0] // local_experts
-    slot_count = received.shape[1]
-    arranged = received.reshape(senders, local_experts, slot_count, received.shape[2])
-    gate_sum = jnp.einsum("sekd,edf->sekf", arranged, w_gate, preferred_element_type=jnp.float32)
-    up_sum = jnp.einsum("sekd,edf->sekf", arranged, w_up, preferred_element_type=jnp.float32)
-    gate_sum = jnp.minimum(gate_sum, clamp_limit)
-    up_sum = jnp.clip(up_sum, -clamp_limit, clamp_limit)
-    active = (gate_sum * jax.nn.sigmoid(1.702 * gate_sum) * (up_sum + 1.0)).astype(jnp.bfloat16)
-    partial_out = jnp.einsum("sekf,efd->sekd", active, w_down, preferred_element_type=jnp.float32)
-    summed = lax.psum_scatter(
-        partial_out.astype(jnp.bfloat16), "att", scatter_dimension=3, tiled=True
-    )
-    answer = lax.all_to_all(
-        summed.reshape(senders * local_experts, slot_count, -1),
-        "exp",
-        split_axis=0,
-        concat_axis=0,
-        tiled=True,
-    )
-    flat_returned = answer.reshape(expert_count * capacity, -1)
-    picked = flat_returned[slot_index].reshape(decode_row_count, TOP, -1).astype(jnp.float32)
-    shares = weight_codes.astype(jnp.float32)
-    shares = shares / jnp.sum(shares, axis=1, keepdims=True)
-    mixture = jnp.sum(picked * shares[:, :, None], axis=1).astype(jnp.bfloat16)
+    near = lax.axis_size("att") == 2 and lax.axis_size("exp") % 4 == 0 and w_gate.shape[0] == 1
+    experts = ringed_experts if near else routed_experts
+    mixture = experts(hidden, norm_gain, expert_ids, weight_codes, w_gate, w_up, w_down)
     return (attended, mixture)
 
 

time: 316 us -> 196 us (0.62); the launches traced: 311 us -> 195 us
  Pallas kernels: 0 us -> 89.9 us
  blocking collectives: 95.3 us -> 9.99 us
  waiting for transfers between devices: 78 us -> 0.04 us
  matrix products: 53.9 us -> 24.2 us
  starting transfers between devices: 4.7 us -> 0.04 us
  local copies, waits for them, and re-layouts: 51.3 us -> 47.2 us
  other arithmetic: 12.9 us -> 9.4 us
    pallas_call x0 -> x1, Pallas kernels: none -> 89.9 us  [moe(): pl.pallas_call(functools.partial(moe_kernel, n), out_shape=jax.ShapeDtype...]
    all_to_all x1 -> x0, blocking collectives: 74.1 us -> none  [shards(): lax.all_to_all(outgoing, 'exp', split_axis=0, concat_axis=0, tiled=True)]
    unnamed x3 -> x1, waiting for transfers between devices: 40.4 us -> 0.02 us
    all_to_all x1 -> x0, waiting for transfers between devices: 37.5 us -> none  [shards(): lax.all_to_all(summed.reshape(senders * local_experts, slot_count, -1), '...]
    dot_general x3 -> x0, matrix products: 29.9 us -> none  [the longest x1 18.8 us: shards(): jnp.einsum('sekf,efd->sekd', active, w_down, preferred_element_type=jnp.f...]
    all_gather x1 -> x0, blocking collectives: 6.33 us -> none  [shards(): source_rows = lax.all_gather(normed, 'att', axis=1, tiled=True)]
    psum x1 -> x0, blocking collectives: 4.94 us -> none  [shards(): squares = lax.psum(jnp.sum(hidden * hidden, axis=1), 'att')]
    all_to_all x1 -> x0, starting transfers between devices: 4.62 us -> none  [shards(): lax.all_to_all(summed.reshape(senders * local_experts, slot_count, -1), '...]
  transfers between devices with their start and end apart: 3 -> 1, of which waited for: 2 -> 0; matrix products, arithmetic and copies ran while one was open for 5% -> 19% of each run, Pallas kernels for 0% -> 0%
where the time goes in v1:
time: 196 us; the launch traced here: 195 us
  Pallas kernels  89.9 us (46%)
  local copies, waits for them, and re-layouts  47.2 us (24%)
  matrix products  24.2 us (12%)
  between operations  14.3 us (7%)
  blocking collectives  9.99 us (5%)
  other arithmetic  9.4 us (5%)
    pallas_call x1, Pallas kernels, moe(): pl.pallas_call(functools.partial(moe_kernel, n), out_shape=jax.ShapeDtype...  89.9 us
    unnamed x25, local copies, waits for them, and re-layouts  25.7 us
    dot_general x1, matrix products, shards(): projected = jnp.dot(attention, w_out, preferred_element_type=jnp.float32)  10.1 us
    all_gather x2, blocking collectives, combined_all(): lax.all_gather(part.astype(kind), axis)  9.99 us
    dot_general x2, matrix products, local_partials(): jnp.einsum('rgqd,tgd->rgqt', grouped_heads, cached_key_block, preferred_e...  9.02 us
    convert_element_type x1, other arithmetic, local_partials(): weights.astype(jnp.bfloat16)  7.99 us
    dot_general x2, matrix products, local_partials(): jnp.einsum('rgqt,tgd->rgqd', weights.astype(jnp.bfloat16), cached_value_b...  5.06 us
  transfers between devices with their start and end apart: 1, of which 0 were waited for; matrix products, arithmetic and copies ran while one was open for 19% of the time, Pallas kernels for 0%

profile of v1, /device:TPU:0, one launch (start us, length us, event | category | flops | bytes accessed | tf_op | source)
XLA Modules:
  0.0 195.0 jit_solution(14649500145532369281)
XLA Ops:
  7.2 2.5 %fusion.38 = (bf16[1,512,512]{2,1,0:T(8,128)(2,1)S(1)}, bf16[1,512,512]{2,1,0:T(8,128)(2,1)}, bf16[1,512,512]{2,1,0:T(8,128)(2,1)S(1)}, bf16[1,512,512]{2,1,0:T(8,128)(2,1)S(1)}) fusion(bf16[2,512,1024]{2,1,0:T(8,128)(2,1)} %param.15), kind=kLoop, calls=%fused_computation.62 | loop fusion | bytes 4194304 | tf_op jit(solution)/shard_map/slice | solution.py:60
  9.9 2.1 %reshape.279 = bf16[64,8,8,64]{3,2,1,0:T(8,128)(2,1)S(1)} reshape(bf16[64,4096]{1,0:T(8,128)(2,1)} %param.13) | data formatting | bytes 1048576 | tf_op jit(solution)/shard_map/reshape | solution.py:602
  12.0 1.3 copy.113
  13.3 4.5 %bitcast_reduce_fusion = (f32[64,8,8]{0,2,1:T(8,128)S(1)}, f32[8,512,64,8]{1,2,3,0:T(8,128)}) fusion(bf16[512,8,64,1]{0,2,3,1:T(8,128)(2,1)S(1)} %bitcast.129, bf16[64,8,8,64]{3,2,1,0:T(8,128)(2,1)S(1)} %reshape.279), kind=kOutput, calls=%fused_computation.1 | convolution fusion | flops 272625664 | bytes 9453568 | tf_op jit(solution)/shard_map/rgqd,tgd->rgqt/dot_general | solution.py:64
  17.8 4.5 %bitcast_reduce_fusion.1 = (f32[64,8,8]{0,2,1:T(8,128)S(1)}, f32[8,512,64,8]{1,2,3,0:T(8,128)}) fusion(bf16[512,8,64,1]{0,2,3,1:T(8,128)(2,1)S(1)} %bitcast.128, bf16[64,8,8,64]{3,2,1,0:T(8,128)(2,1)S(1)} %reshape.279), kind=kOutput, calls=%fused_computation.4 | convolution fusion | flops 272625664 | bytes 9453568 | tf_op jit(solution)/shard_map/rgqd,tgd->rgqt/dot_general | solution.py:64
  22.7 8.0 %fusion.3 = (bf16[64,8,8,512]{3,0,2,1:T(8,128)(2,1)S(1)}, bf16[64,8,8]{0,2,1:T(8,128)(2,1)S(1)}, bf16[64,8,8]{0,2,1:T(8,128)(2,1)S(1)}, bf16[64,8,8,512]{3,0,2,1:T(8,128)(2,1)S(1)}) fusion(f32[8,512,64,8]{1,2,3,0:T(8,128)} %get-tuple-element.56, f32[64,8,8]{0,2,1:T(8,128)S(1)} %get-tuple-element.55, f32[64,8,8]{0,2,1:T(8,128)S(1)} %get-tuple-element.53, ...), kind=kLoop, calls=%fused_computation.7 | loop fusion | flops 16769024 | bytes 25214976 | tf_op jit(solution)/shard_map/convert_element_type | solution.py:77
  30.7 2.4 %fusion.6 = bf16[8,64,8,64]{3,2,1,0:T(8,128)(2,1)S(1)} fusion(bf16[512,8,64,1]{0,2,3,1:T(8,128)(2,1)S(1)} %bitcast.130, bf16[64,8,8,512]{3,0,2,1:T(8,128)(2,1)S(1)} %get-tuple-element.59), kind=kOutput, calls=%fused_computation.10 | convolution fusion | flops 268435456 | bytes 5242880 | tf_op jit(solution)/shard_map/rgqt,tgd->rgqd/dot_general | solution.py:75
  33.2 2.6 %fusion.12 = bf16[64,8,8,64]{3,2,0,1:T(8,128)(2,1)S(1)} fusion(bf16[8,64,8,64]{3,2,1,0:T(8,128)(2,1)S(1)} %fusion.6, bf16[512,8,64,1]{0,2,3,1:T(8,128)(2,1)S(1)} %bitcast.131, bf16[64,8,8,512]{3,0,2,1:T(8,128)(2,1)S(1)} %get-tuple-element.18, pred[64]{0:T(512)(128)(4,1)S(1)} %broadcast_compare_fusion), kind=kOutput, calls=%fused_computation.17 | convolution fusion | flops 268697600 | bytes 5767232 | tf_op jit(solution)/shard_map/rgqt,tgd->rgqd/dot_general | solution.py:75
  36.1 1.6 convert_element_type.175
  37.9 5.4 %all_gather.13 = bf16[2,64,64]{2,1,0:T(8,128)(2,1)S(1)} all-gather(bf16[1,64,64]{2,1,0:T(8,128)(2,1)S(1)} %copy.122), channel_id=1, replica_groups=mesh['groups'=2,'att'=2,'exp'=8] {'att'}, dimensions={0}, use_global_device_ids=true | all-gather | bytes 24576 | tf_op jit(solution)/shard_map/all_gather | solution.py:24
  43.5 4.6 %all_gather.14 = bf16[2,64,64]{2,1,0:T(8,128)(2,1)S(1)} all-gather(bf16[1,64,64]{2,1,0:T(8,128)(2,1)S(1)} %copy.130), channel_id=1, replica_groups=mesh['groups'=2,'att'=2,'exp'=8] {'att'}, dimensions={0}, use_global_device_ids=true | all-gather | bytes 24576 | tf_op jit(solution)/shard_map/all_gather | solution.py:24
  48.5 0.6 multiply_reduce_fusion
  50.1 0.7 div.20
  51.4 1.6 mul.133
  53.7 1.6 mul.136
  56.1 1.6 mul.144
  58.4 1.6 mul.147
  60.4 1.6 reshape.280
  62.0 11.7 %copy.134.wg_hbm = bf16[1,2880,1440]{2,1,0:T(8,128)(2,1)} copy(bf16[1,2880,1440]{1,2,0:T(8,128)(2,1)} %param.23) | data formatting | bytes 16588800 | tf_op args[10]
  73.8 11.9 %copy.135.wu_hbm = bf16[1,2880,1440]{2,1,0:T(8,128)(2,1)} copy(bf16[1,2880,1440]{1,2,0:T(8,128)(2,1)} %param.24) | data formatting | bytes 16588800 | tf_op args[11]
  85.8 10.1 %multiply_reduce_fusion.1 = (f32[64]{0:T(128)S(1)}, bf16[64,1440]{1,0:T(8,128)(2,1)}, bf16[64,1440]{1,0:T(8,128)(2,1)}) fusion(f32[1440]{0:T(1024)S(1)} %convert_element_type.197, bf16[4096,1440]{0,1:T(8,128)(2,1)} %param.18, f32[64,4096]{1,0:T(8,128)S(1)} %div.20, f32[64,4096]{1,0:T(8,128)} %mul.147, f32[64,4096]{1,0:T(8,128)} %reshape.280, ...), kind=kOutput, calls=%fused_computation.31 | convolution fusion | flops 758241216 | bytes 19695488 | tf_op jit(solution)/shard_map/dot_general | solution.py:608
  96.1 0.6 pad_maximum_fusion.meta_ref
  96.7 89.9 %shard_map.140 = bf16[64,1440]{1,0:T(8,128)(2,1)} custom-call(bf16[64,1440]{1,0:T(8,128)(2,1)} %get-tuple-element.35.u_ref, f32[8,128]{1,0:T(8,128)} %pad_maximum_fusion.meta_ref, bf16[1,2880,1440]{2,1,0:T(8,128)(2,1)} %copy.134.wg_hbm, bf16[1,2880,1440]{2,1,0:T(8,128)(2,1)} %copy.135.wu_hbm, bf16[1,1440,2880]{2,1,0:T(8,128)(2,1)} %wd_hbm.1), custom_call_target="tpu_custom_call" | custom-call | tf_op jit(solution)/shard_map/pallas_call | solution.py:480
  186.6 1.6 copy.161
  (56 shorter events, 5.9 us)
Async XLA Ops:
  7.2 78.6 %all-gather.2.cloned.1.call-start = ((), (), s32[]{:S(2)}) async-start(), calls=%async_computation | async-start | bytes 1572864 | tf_op jit(solution)/shard_map/all_gather | solution.py:24
  13.3 9.0 %copy-start.8 = (s32[64]{0:T(128)S(1)}, s32[64]{0:T(128)}, u32[]{:S(2)}) copy-start(s32[64]{0:T(128)} %param.16) | copy-start | bytes 772
  33.2 15.2 %copy-start.3 = (bf16[64,1024]{1,0:T(8,128)(2,1)S(1)}, bf16[64,1024]{1,0:T(8,128)(2,1)}, u32[]{:S(2)}) copy-start(bf16[64,1024]{1,0:T(8,128)(2,1)} %param.14) | copy-start | bytes 393220
  33.2 16.1 %copy-start.7 = (f32[64]{0:T(128)S(1)}, f32[64]{0:T(128)}, u32[]{:S(2)}) copy-start(f32[64]{0:T(128)} %param.17) | copy-start | bytes 772
  55.4 6.7 %copy-start.5 = (bf16[1440]{0:T(1024)(128)(2,1)S(1)}, bf16[1440]{0:T(1024)(128)(2,1)}, u32[]{:S(2)}) copy-start(bf16[1440]{0:T(1024)(128)(2,1)} %param.20) | copy-start | bytes 8644
  73.8 12.0 %copy-start.4 = (s32[64,4]{0,1:T(4,128)S(1)}, s32[64,4]{0,1:T(4,128)}, u32[]{:S(2)}) copy-start(s32[64,4]{0,1:T(4,128)} %param.22) | copy-start | bytes 3076
  73.8 12.0 %copy-start.6 = (s32[64,4]{0,1:T(4,128)S(1)}, s32[64,4]{0,1:T(4,128)}, u32[]{:S(2)}) copy-start(s32[64,4]{0,1:T(4,128)} %param.21) | copy-start | bytes 3076
  73.8 12.1 %copy-start = (f32[64,4096]{1,0:T(8,128)S(1)}, f32[64,4096]{1,0:T(8,128)}, u32[]{:S(2)}) copy-start(f32[64,4096]{1,0:T(8,128)} %mul.133) | copy-start | bytes 3145732
  73.8 12.1 %copy-start.1 = (f32[64,4096]{1,0:T(8,128)S(1)}, f32[64,4096]{1,0:T(8,128)}, u32[]{:S(2)}) copy-start(f32[64,4096]{1,0:T(8,128)} %mul.136) | copy-start | bytes 3145732
  73.8 12.1 %copy-start.2 = (bf16[64,1440]{1,0:T(8,128)(2,1)S(1)}, bf16[64,1440]{1,0:T(8,128)(2,1)}, u32[]{:S(2)}) copy-start(bf16[64,1440]{1,0:T(8,128)(2,1)} %param.19) | copy-start | bytes 552964
Sparse Core Ops, SparseCore 0:
  37.9 23.9 all-gather.1

commit v2 on v1

--- a/solution.py
+++ b/solution.py
@@ -16,6 +16,7 @@
 
 
 MESH = pl.DeviceIdType.MESH
+NT = (((1,), (1,)), ((), ()))
 clamp_limit = 7.0
 
 
@@ -131,14 +132,33 @@
         .astype(jnp.bfloat16)
     )
 
-def moe_kernel(
+def layer_kernel(
     n,
-    u_ref,
-    meta_ref,
+    q_ref,
+    kv_ref,
+    branch_ref,
+    sink_ref,
+    residual_ref,
+    gain_ref,
+    share_ref,
+    cache_hbm,
+    wo_hbm,
     wg_hbm,
     wu_hbm,
     wd_hbm,
+    attended_ref,
     out_ref,
+    cache,
+    wo,
+    hidden_t,
+    OS,
+    OR,
+    TS,
+    TR,
+    osend,
+    orecv,
+    tsend,
+    trecv,
     wg,
     wu,
     wd,
@@ -167,10 +187,10 @@
 ):
     rings = n // 2
     half_ring = rings // 2
-    rows = u_ref.shape[0]
-    width = u_ref.shape[1]
+    rows = residual_ref.shape[0]
+    width = residual_ref.shape[1]
     half_rows = rows // 2
-    experts = meta_ref.shape[0]
+    experts = share_ref.shape[0]
     a = lax.axis_index("att")
     e = lax.axis_index("exp")
     z = e // 2
@@ -187,6 +207,10 @@
     mate = {"exp": z * 2 + 1 - c}
     across = {"att": 1 - a}
 
+    cache_load = pltpu.make_async_copy(cache_hbm, cache, wsem.at[3])
+    cache_load.start()
+    wo_load = pltpu.make_async_copy(wo_hbm, wo, wsem.at[4])
+    wo_load.start()
     loads = [
         pltpu.make_async_copy(wg_hbm.at[0], wg, wsem.at[0]),
         pltpu.make_async_copy(wu_hbm.at[0], wu, wsem.at[1]),
@@ -199,6 +223,133 @@
     for target in (right, left, mate, across):
         pl.semaphore_signal(barrier, inc=1, device_id=target, device_id_type=MESH)
     pl.semaphore_wait(barrier, 4)
+    eye = lax.broadcasted_iota(jnp.int32, (rows, rows), 0) == lax.broadcasted_iota(
+        jnp.int32, (rows, rows), 1
+    )
+
+    per = QUERY_HEADS // KEY_VALUE_HEADS
+    columns = per * rows
+    pair = 2 * HEAD_SIZE
+    pairs = KEY_VALUE_HEADS // 2
+    kv_width = KEY_VALUE_HEADS * HEAD_SIZE
+    second_context = branch_ref[...] == 1
+
+    def transposed_queries(g2):
+        start = pl.multiple_of(g2 * 2 * per * HEAD_SIZE, 128)
+        block = q_ref[:, pl.ds(start, 2 * per * HEAD_SIZE)].astype(jnp.float32).T
+        block = block * HEAD_SIZE ** (-0.5)
+
+        def head(k):
+            return block[k * HEAD_SIZE : (k + 1) * HEAD_SIZE]
+
+        return [
+            jnp.concatenate([head(j * per + h) for h in range(per)], axis=1) for j in range(2)
+        ]
+
+    def parts_copies(g2):
+        return (
+            pltpu.make_async_remote_copy(
+                src_ref=OS.at[g2],
+                dst_ref=OR.at[g2],
+                send_sem=osend.at[g2],
+                recv_sem=orecv.at[g2],
+                device_id=across,
+                device_id_type=MESH,
+            ),
+            pltpu.make_async_remote_copy(
+                src_ref=TS.at[g2],
+                dst_ref=TR.at[g2],
+                send_sem=tsend.at[g2],
+                recv_sem=trecv.at[g2],
+                device_id=across,
+                device_id_type=MESH,
+            ),
+        )
+
+    cache_load.wait()
+
+    @pl.loop(0, pairs)
+    def _(g2):
+        heads_t = transposed_queries(g2)
+        key_cols = pl.ds(pl.multiple_of(g2 * pair, 128), pair)
+        value_cols = pl.ds(pl.multiple_of(kv_width + g2 * pair, 128), pair)
+        keys = jnp.concatenate([cache[0, :, key_cols], cache[1, :, key_cols]], axis=1)
+        values_t = [cache[k, :, value_cols].T for k in range(2)]
+        for j in range(2):
+            q = heads_t[j]
+            none = jnp.zeros_like(q)
+            first_q = jnp.where(second_context, 0.0, q)
+            second_q = jnp.where(second_context, q, 0.0)
+            stack = [first_q, none, second_q, none] if j == 0 else [none, first_q, none, second_q]
+            stacked = jnp.concatenate(stack, axis=0).astype(jnp.bfloat16)
+            scores = jnp.dot(keys, stacked, preferred_element_type=jnp.float32)
+            top = jnp.max(scores, axis=0, keepdims=True)
+            weights = jnp.exp(scores - top)
+            total = jnp.sum(weights, axis=0, keepdims=True)
+            own_rows = slice(j * HEAD_SIZE, (j + 1) * HEAD_SIZE)
+            values = jnp.concatenate([v[own_rows] for v in values_t], axis=0)
+            out = jnp.dot(
+                values, weights.astype(jnp.bfloat16), preferred_element_type=jnp.float32
+            )
+            out = jnp.where(second_context, out[HEAD_SIZE:], out[:HEAD_SIZE])
+            OS[g2, own_rows, :] = out.astype(jnp.bfloat16)
+            TS[g2, 2 * j : 2 * j + 1, :] = top
+            TS[g2, 2 * j + 1 : 2 * j + 2, :] = total
+        for copy in parts_copies(g2):
+            copy.start()
+
+    hidden_t[...] = jnp.zeros_like(hidden_t)
+    wo_load.wait()
+
+    @pl.loop(0, pairs)
+    def _(g2):
+        heads_t = transposed_queries(g2)
+        key_cols = pl.ds(pl.multiple_of(g2 * pair, 128), pair)
+        value_cols = pl.ds(pl.multiple_of(kv_width + g2 * pair, 128), pair)
+        own_keys = kv_ref[:, key_cols].astype(jnp.float32).T
+        own_values = kv_ref[:, value_cols].astype(jnp.float32).T
+        sinks = sink_ref[g2]
+        for copy in parts_copies(g2):
+            copy.wait()
+        mine, theirs = TS[g2], TR[g2]
+        stacked = []
+        for j in range(2):
+            own_rows = slice(j * HEAD_SIZE, (j + 1) * HEAD_SIZE)
+            own_key = jnp.concatenate([own_keys[own_rows]] * per, axis=1)
+            own_value = jnp.concatenate([own_values[own_rows]] * per, axis=1)
+            own_score = jnp.sum(heads_t[j] * own_key, axis=0, keepdims=True)
+            sink = sinks[j : j + 1]
+            top_a, top_b = mine[2 * j : 2 * j + 1], theirs[2 * j : 2 * j + 1]
+            peak = jnp.maximum(jnp.maximum(top_a, top_b), jnp.maximum(own_score, sink))
+            factor_a = jnp.exp(top_a - peak)
+            factor_b = jnp.exp(top_b - peak)
+            own_factor = jnp.exp(own_score - peak)
+            denominator = (
+                mine[2 * j + 1 : 2 * j + 2] * factor_a
+                + theirs[2 * j + 1 : 2 * j + 2] * factor_b
+                + own_factor
+                + jnp.exp(sink - peak)
+            )
+            out = (
+                OS[g2, own_rows, :].astype(jnp.float32) * factor_a
+                + OR[g2, own_rows, :].astype(jnp.float32) * factor_b
+                + own_factor * own_value
+            ) / denominator
+            stacked += [out[:, h * rows : (h + 1) * rows] for h in range(per)]
+        attention_t = jnp.concatenate(stacked, axis=0).astype(jnp.bfloat16)
+        cols = pl.ds(pl.multiple_of(g2 * 2 * per * HEAD_SIZE, 128), 2 * per * HEAD_SIZE)
+        hidden_t[...] += jnp.dot(wo[:, cols], attention_t, preferred_element_type=jnp.float32)
+
+    hidden = hidden_t[...].T + residual_ref[...].astype(jnp.float32)
+    attended_ref[...] = hidden.astype(jnp.bfloat16)
+    squares = jnp.sum(hidden * hidden, axis=1, keepdims=True)
+    squares = jnp.sum(
+        jnp.where(eye, jnp.broadcast_to(squares, (rows, rows)), 0.0), axis=0, keepdims=True
+    )
+    META[a, e] = jnp.concatenate(
+        [share_ref[...], jnp.broadcast_to(squares, (experts, rows))], axis=1
+    )
+    X[a, e] = (hidden * gain_ref[...].astype(jnp.float32)).astype(jnp.bfloat16)
 
     pending = []
     counter = [0]
@@ -256,12 +407,8 @@
             ).wait_recv()
 
     halves = (a, 1 - a)
-    send(u_ref, meta_ref, a, e, across)
-    send(u_ref, meta_ref, a, e, right)
-    send(u_ref, meta_ref, a, e, left)
-    send(u_ref, meta_ref, a, e, mate)
-    X[a, e] = u_ref[...]
-    META[a, e] = meta_ref[...]
+    for target in (across, right, left, mate):
+        send(X.at[a, e], META.at[a, e], a, e, target)
     arrived(1 - a, e)
     own = (1 - a, e)
     for target in (right, left, mate):
@@ -295,18 +442,15 @@
         if 0 < step < half_ring:
             arrived(h, at(step) * 2 + 1 - c)
 
-    eye = lax.broadcasted_iota(jnp.int32, (rows, rows), 0) == lax.broadcasted_iota(
-        jnp.int32, (rows, rows), 1
-    )
-
     def upright(row):
         return jnp.sum(jnp.where(eye, jnp.broadcast_to(row, (rows, rows)), 0.0), axis=1, keepdims=True)
 
     def run_chunk(offsets):
         blocks = [at(o) * 2 + k for o in offsets for k in range(2)]
         count = len(blocks) * rows
-        x0 = jnp.concatenate([X[0, b] for b in blocks], axis=0)
-        x1 = jnp.concatenate([X[1, b] for b in blocks], axis=0)
+        x = jnp.concatenate(
+            [jnp.concatenate([X[0, b], X[1, b]], axis=1) for b in blocks], axis=0
+        )
         shares, inverses = [], []
         pick = lax.broadcasted_iota(jnp.int32, (experts, 2 * rows), 0) == e
         for b in blocks:
@@ -319,10 +463,8 @@
 
         def first(start, size):
             cols = pl.ds(start, size)
-            g = jnp.dot(x0, wg[:width, cols], preferred_element_type=jnp.float32)
-            g += jnp.dot(x1, wg[width:, cols], preferred_element_type=jnp.float32)
-            u = jnp.dot(x0, wu[:width, cols], preferred_element_type=jnp.float32)
-            u += jnp.dot(x1, wu[width:, cols], preferred_element_type=jnp.float32)
+            g = lax.dot_general(x, wg[cols, :], NT, preferred_element_type=jnp.float32)
+            u = lax.dot_general(x, wu[cols, :], NT, preferred_element_type=jnp.float32)
             g = jnp.minimum(g * inverse, clamp_limit)
             u = jnp.clip(u * inverse, -clamp_limit, clamp_limit)
             act_ref[:, cols] = (g * jax.nn.sigmoid(1.702 * g) * (u + 1.0)).astype(jnp.bfloat16)
@@ -466,26 +608,41 @@
     out_ref[...] = (mine + YR[...].astype(jnp.float32)).astype(jnp.bfloat16)
 
 
-def moe(u, meta, w_gate, w_up, w_down):
+def layer(
+    queries, row_key_value, cache, branch, sinks, w_out, residual, gain, by_expert, w_gate, w_up, w_down
+):
     n = lax.axis_size("exp")
     rings = n // 2
     half_ring = max(1, rings // 2)
-    rows, width = u.shape
+    rows, width = residual.shape
+    per = QUERY_HEADS // KEY_VALUE_HEADS
+    pairs = KEY_VALUE_HEADS // 2
     full = 2 * width
-    experts = meta.shape[0]
+    experts = by_expert.shape[0]
     per_chunk = 4 * rows
     sends = 4 * n + 8
     bf = jnp.bfloat16
     dma = pltpu.SemaphoreType.DMA
     return pl.pallas_call(
-        functools.partial(moe_kernel, n),
-        out_shape=jax.ShapeDtypeStruct((rows, width), bf),
-        in_specs=[pl.BlockSpec(memory_space=pltpu.VMEM)] * 2
-        + [pl.BlockSpec(memory_space=pl.ANY)] * 3,
-        out_specs=pl.BlockSpec(memory_space=pltpu.VMEM),
+        functools.partial(layer_kernel, n),
+        out_shape=[jax.ShapeDtypeStruct((rows, width), bf)] * 2,
+        in_specs=[pl.BlockSpec(memory_space=pltpu.VMEM)] * 7
+        + [pl.BlockSpec(memory_space=pl.ANY)] * 5,
+        out_specs=[pl.BlockSpec(memory_space=pltpu.VMEM)] * 2,
         scratch_shapes=[
-            pltpu.VMEM((full, width), bf),
-            pltpu.VMEM((full, width), bf),
+            pltpu.VMEM(cache.shape, bf),
+            pltpu.VMEM((width, QUERY_HEADS * HEAD_SIZE), bf),
+            pltpu.VMEM((width, rows), jnp.float32),
+            pltpu.VMEM((pairs, 2 * HEAD_SIZE, per * rows), bf),
+            pltpu.VMEM((pairs, 2 * HEAD_SIZE, per * rows), bf),
+            pltpu.VMEM((pairs, 8, per * rows), jnp.float32),
+            pltpu.VMEM((pairs, 8, per * rows), jnp.float32),
+            dma((pairs,)),
+            dma((pairs,)),
+            dma((pairs,)),
+            dma((pairs,)),
+            pltpu.VMEM((width, full), bf),
+            pltpu.VMEM((width, full), bf),
             pltpu.VMEM((width, full), bf),
             pltpu.VMEM((2, n, rows, width), bf),
             pltpu.VMEM((2, n, experts, 2 * rows), jnp.float32),
@@ -498,7 +655,7 @@
             pltpu.VMEM((half_ring, rows, full), bf),
             pltpu.VMEM((rows, width), bf),
             pltpu.VMEM((rows, width), bf),
-            dma((3,)),
+            dma((5,)),
             dma((sends,)),
             dma((2, n, 2)),
             dma((sends,)),
@@ -513,22 +670,27 @@
         compiler_params=pltpu.CompilerParams(
             collective_id=1, has_side_effects=True, vmem_limit_bytes=62 * 1024 * 1024
         ),
-    )(u, meta, w_gate, w_up, w_down)
-
-
-def ringed_experts(hidden, norm_gain, expert_ids, weight_codes, w_gate, w_up, w_down):
-    rows = hidden.shape[0]
-    squares = jnp.sum(hidden * hidden, axis=1)
-    scaled = (hidden * norm_gain.astype(jnp.float32)[None, :]).astype(jnp.bfloat16)
-    expert_count = w_gate.shape[0] * lax.axis_size("exp")
+    )(
+        queries,
+        row_key_value,
+        jnp.tile(branch, per)[None, :],
+        jnp.repeat(sinks, rows).reshape(pairs, 2, per * rows),
+        residual,
+        gain[None, :],
+        by_expert,
+        cache,
+        w_out.T,
+        jnp.swapaxes(w_gate, 1, 2),
+        jnp.swapaxes(w_up, 1, 2),
+        w_down,
+    )
+
+
+def share_table(expert_ids, weight_codes, expert_count):
     shares = weight_codes.astype(jnp.float32)
     shares = shares / jnp.sum(shares, axis=1, keepdims=True)
     named = expert_ids[None, :, :] == jnp.arange(expert_count, dtype=jnp.int32)[:, None, None]
-    by_expert = jnp.sum(jnp.where(named, shares[None], 0.0), axis=2)
-    meta = jnp.concatenate(
-        [by_expert, jnp.broadcast_to(squares[None, :], (expert_count, rows))], axis=1
-    )
-    return moe(scaled, meta, w_gate, w_up, w_down)
+    return jnp.sum(jnp.where(named, shares[None], 0.0), axis=2)
 
 
 def routed_experts(hidden, norm_gain, expert_ids, weight_codes, w_gate, w_up, w_down):
@@ -598,6 +760,22 @@
     w_up,
     w_down,
 ):
+    near = lax.axis_size("att") == 2 and lax.axis_size("exp") % 4 == 0 and w_gate.shape[0] == 1
+    if near:
+        return layer(
+            queries,
+            row_key_value,
+            shared_context_cache,
+            branch,
+            sink_logits,
+            w_out,
+            residual,
+            norm_gain,
+            share_table(expert_ids, weight_codes, w_gate.shape[0] * lax.axis_size("exp")),
+            w_gate,
+            w_up,
+            w_down,
+        )
     decode_row_count = queries.shape[0]
     grouped_heads = queries.reshape(
         decode_row_count, KEY_VALUE_HEADS, QUERY_HEADS // KEY_VALUE_HEADS, HEAD_SIZE
@@ -608,9 +786,9 @@
     projected = jnp.dot(attention, w_out, preferred_element_type=jnp.float32)
     hidden = residual.astype(jnp.float32) + projected
     attended = hidden.astype(jnp.bfloat16)
-    near = lax.axis_size("att") == 2 and lax.axis_size("exp") % 4 == 0 and w_gate.shape[0] == 1
-    experts = ringed_experts if near else routed_experts
-    mixture = experts(hidden, norm_gain, expert_ids, weight_codes, w_gate, w_up, w_down)
+    mixture = routed_experts(
+        hidden, norm_gain, expert_ids, weight_codes, w_gate, w_up, w_down
+    )
     return (attended, mixture)
 
 

time: 196 us -> 121 us (0.62)
  local copies, waits for them, and re-layouts: 47.2 us -> 7.32 us
  matrix products: 24.2 us -> 0 us
  Pallas kernels: 89.9 us -> 110 us
  between operations: 14.3 us -> 0.64 us
  blocking collectives: 9.99 us -> 0 us
  other arithmetic: 9.4 us -> 2.66 us
    dot_general x5 -> x0, matrix products: 24.2 us -> none  [the longest x1 10.1 us: shards(): projected = jnp.dot(attention, w_out, preferred_element_type=jnp.float32)]
    unnamed x25 -> x2, local copies, waits for them, and re-layouts: 25.7 us -> 3.23 us
    pallas_call x1, Pallas kernels: 89.9 us -> 110 us  [layer(): pl.pallas_call(functools.partial(layer_kernel, n), out_shape=[jax.ShapeDt...]
    all_gather x2 -> x0, blocking collectives: 9.99 us -> none  [combined_all(): lax.all_gather(part.astype(kind), axis)]
    mul x8 -> x0, local copies, waits for them, and re-layouts: 8.99 us -> none  [the longest x2 2.25 us: merge_parts(): first_out.reshape(decode_row_count, head_count, -1)]
    convert_element_type x4 -> x0, other arithmetic: 8.02 us -> none  [the longest x1 7.99 us: local_partials(): weights.astype(jnp.bfloat16)]
    slice x7 -> x0, local copies, waits for them, and re-layouts: 4.41 us -> none  [the longest x3 2.94 us: local_partials(): shared_context_cache[context_slot, :, KEY_VALUE_HEADS * HEAD_SIZE:]]
    reshape x2 -> x0, local copies, waits for them, and re-layouts: 3.69 us -> none  [the longest x1 2.06 us: shards(): queries.reshape(decode_row_count, KEY_VALUE_HEADS, QUERY_HEADS // KEY_VAL...]
  transfers between devices with their start and end apart: 1 -> 0, of which waited for: 0 -> 0; matrix products, arithmetic and copies ran while one was open for 19% -> 0% of each run, Pallas kernels for 0% -> 0%
where the time goes in v2:
time: 121 us; the launch traced here: 120 us
  Pallas kernels  110 us (91%)
  local copies, waits for them, and re-layouts  7.32 us (6%)
  other arithmetic  2.66 us (2%)
    pallas_call x1, Pallas kernels, layer(): pl.pallas_call(functools.partial(layer_kernel, n), out_shape=[jax.ShapeDt...  110 us
    unnamed x2, local copies, waits for them, and re-layouts  3.23 us

profile of v2, /device:TPU:0, one launch (start us, length us, event | category | flops | bytes accessed | tf_op | source)
XLA Modules:
  0.0 120.4 jit_solution(12027733060011343001)
XLA Ops:
  0.6 0.7 convert_reduce_fusion
  1.3 0.7 convert_divide_fusion
  2.0 1.3 %select_reduce_fusion.share_ref = f32[8,64]{1,0:T(8,128)} fusion(f32[64,4]{0,1:T(4,128)S(1)} %convert_divide_fusion, s32[64,4]{0,1:T(4,128)} %param.21), kind=kLoop, calls=%fused_computation | loop fusion | flops 5632 | bytes 4096 | tf_op jit(solution)/shard_map/reduce_sum | solution.py:693
  3.3 0.7 tile.2
  3.9 0.6 broadcast_in_dim_tile.3.branch_ref
  4.6 0.7 broadcast_in_dim.26
  5.3 1.3 %broadcast_in_dim.29.gain_ref = bf16[1,1440]{1,0:T(2,128)(2,1)} reshape(bf16[1440]{0:T(1024)(128)(2,1)} %param.20) | data formatting | bytes 5760 | tf_op jit(solution)/shard_map/broadcast_in_dim | solution.py:679
  6.6 0.1 broadcast_in_dim.27
  6.7 0.7 broadcast_in_dim.28.sink_ref
  7.4 109.8 %shard_map.140 = (bf16[64,1440]{1,0:T(8,128)(2,1)}, bf16[64,1440]{1,0:T(8,128)(2,1)}) custom-call(bf16[64,4096]{1,0:T(8,128)(2,1)} %q_ref.1, bf16[64,1024]{1,0:T(8,128)(2,1)} %kv_ref.1, s32[1,512]{1,0:T(1,128)} %broadcast_in_dim_tile.3.branch_ref, f32[4,2,512]{2,1,0:T(2,128)} %broadcast_in_dim.28.sink_ref, bf16[64,1440]{1,0:T(8,128)(2,1)} %residual_ref.1, ...), custom_call_target="tpu_custom_call" | custom-call | tf_op jit(solution)/shard_map/pallas_call | solution.py:626
  117.2 1.6 %copy.19 = bf16[64,1440]{1,0:T(8,128)(2,1)} copy(bf16[64,1440]{1,0:T(8,128)(2,1)} %get-tuple-element.4) | data formatting | bytes 368640
  118.8 1.6 %copy.20 = bf16[64,1440]{1,0:T(8,128)(2,1)} copy(bf16[64,1440]{1,0:T(8,128)(2,1)} %get-tuple-element.5) | data formatting | bytes 368640

commit v3 on v2

--- a/solution.py
+++ b/solution.py
@@ -167,10 +167,9 @@
     act_ref,
     P_ref,
     CS,
-    SR,
-    SL,
-    RR,
-    RL,
+    KEEP,
+    ZS,
+    ZR,
     YS,
     YR,
     wsem,
@@ -186,24 +185,21 @@
     yrecv,
 ):
     rings = n // 2
-    half_ring = rings // 2
     rows = residual_ref.shape[0]
     width = residual_ref.shape[1]
-    half_rows = rows // 2
     experts = share_ref.shape[0]
     a = lax.axis_index("att")
     e = lax.axis_index("exp")
     z = e // 2
     c = e % 2
 
-    def at(offset):
-        return lax.rem(z + offset + rings, rings)
-
-    def lane(offset):
-        return at(offset) * 2 + c
-
-    right = {"exp": lane(1)}
-    left = {"exp": lane(-1)}
+    pair_count = rings // 2
+    side = z % 2
+    groups_of_chips = []
+    for k in range(pair_count):
+        base = lax.rem(z // 2 + k, pair_count) * 2
+        groups_of_chips.append([base + side, base + 1 - side] if k == 0 else [base + 1 - side, base + side])
+    others = [chip for group in groups_of_chips for chip in group][1:]
     mate = {"exp": z * 2 + 1 - c}
     across = {"att": 1 - a}
 
@@ -220,9 +216,9 @@
         load.start()
 
     barrier = pltpu.get_barrier_semaphore()
-    for target in (right, left, mate, across):
+    for target in [mate, across] + [{"exp": chip * 2 + c} for chip in others]:
         pl.semaphore_signal(barrier, inc=1, device_id=target, device_id_type=MESH)
-    pl.semaphore_wait(barrier, 4)
+    pl.semaphore_wait(barrier, rings + 1)
     eye = lax.broadcasted_iota(jnp.int32, (rows, rows), 0) == lax.broadcasted_iota(
         jnp.int32, (rows, rows), 1
     )
@@ -354,99 +350,57 @@
     pending = []
     counter = [0]
 
-    def send(src_x, src_m, h, idx, target, part=None):
+    def send(h, idx, target):
         k = counter[0]
         counter[0] += 1
-        if part is None:
-            dst_x, slot = X.at[h, idx], 0
-        else:
-            dst_x, slot = X.at[h, idx, pl.ds(part * half_rows, half_rows)], part
-        x_copy = pltpu.make_async_remote_copy(
-            src_ref=src_x,
-            dst_ref=dst_x,
-            send_sem=xsend.at[k],
-            recv_sem=xrecv.at[h, idx, slot],
-            device_id=target,
-            device_id_type=MESH,
-        )
-        x_copy.start()
-        pending.append(x_copy)
-        if part is None or part == 0:
-            m_copy = pltpu.make_async_remote_copy(
-                src_ref=src_m,
-                dst_ref=META.at[h, idx],
-                send_sem=msend.at[k],
-                recv_sem=mrecv.at[h, idx],
+        for ref, sent, received in ((X, xsend, xrecv), (META, msend, mrecv)):
+            copy = pltpu.make_async_remote_copy(
+                src_ref=ref.at[h, idx],
+                dst_ref=ref.at[h, idx],
+                send_sem=sent.at[k],
+                recv_sem=received.at[h, idx],
                 device_id=target,
                 device_id_type=MESH,
             )
-            m_copy.start()
-            pending.append(m_copy)
-
-    def arrived(h, idx, part=None):
-        if part is None:
-            ref, slot = X.at[h, idx], 0
-        else:
-            ref, slot = X.at[h, idx, pl.ds(part * half_rows, half_rows)], part
-        pltpu.make_async_remote_copy(
-            src_ref=ref,
-            dst_ref=ref,
-            send_sem=xsend.at[0],
-            recv_sem=xrecv.at[h, idx, slot],
-            device_id=mate,
-            device_id_type=MESH,
-        ).wait_recv()
-        if part is None or part == 0:
+            copy.start()
+            pending.append(copy)
+
+    def arrived(h, idx):
+        for ref, sent, received in ((X, xsend, xrecv), (META, msend, mrecv)):
             pltpu.make_async_remote_copy(
-                src_ref=META.at[h, idx],
-                dst_ref=META.at[h, idx],
-                send_sem=msend.at[0],
-                recv_sem=mrecv.at[h, idx],
+                src_ref=ref.at[h, idx],
+                dst_ref=ref.at[h, idx],
+                send_sem=sent.at[0],
+                recv_sem=received.at[h, idx],
                 device_id=mate,
                 device_id_type=MESH,
             ).wait_recv()
 
-    halves = (a, 1 - a)
-    for target in (across, right, left, mate):
-        send(X.at[a, e], META.at[a, e], a, e, target)
-    arrived(1 - a, e)
-    own = (1 - a, e)
-    for target in (right, left, mate):
-        send(X.at[own], META.at[own], 1 - a, e, target)
-
-    def forward(step, h):
-        from_left, from_right = lane(-step), lane(step)
-        if step < half_ring:
-            last = step + 1 == half_ring
-            arrived(h, from_left)
-            if last:
-                lo = pl.ds(0, half_rows)
-                send(X.at[h, from_left, lo], META.at[h, from_left], h, from_left, right, 0)
-            else:
-                send(X.at[h, from_left], META.at[h, from_left], h, from_left, right)
-            arrived(h, from_right)
-            if last:
-                hi = pl.ds(half_rows, half_rows)
-                send(X.at[h, from_right, hi], None, h, from_right, left, 1)
-            else:
-                send(X.at[h, from_right], META.at[h, from_right], h, from_right, left)
-            send(X.at[h, from_left], META.at[h, from_left], h, from_left, mate)
-            send(X.at[h, from_right], META.at[h, from_right], h, from_right, mate)
-        else:
-            arrived(h, from_left, 0)
-            arrived(h, from_left, 1)
-            send(X.at[h, from_left], META.at[h, from_left], h, from_left, mate)
-
-    def mates(step, h):
-        arrived(h, at(-step) * 2 + 1 - c)
-        if 0 < step < half_ring:
-            arrived(h, at(step) * 2 + 1 - c)
+    send(a, e, across)
+    for chip in others:
+        send(a, e, {"exp": chip * 2 + c})
+    send(a, e, mate)
+
+    def pass_on(chip):
+        idx = chip * 2 + c
+        arrived(a, idx)
+        send(a, idx, across)
+        send(a, idx, mate)
+
+    def crossed(chip):
+        idx = chip * 2 + c
+        arrived(1 - a, idx)
+        send(1 - a, idx, mate)
+
+    def mates(chip):
+        for h in (a, 1 - a):
+            arrived(h, chip * 2 + 1 - c)
 
     def upright(row):
         return jnp.sum(jnp.where(eye, jnp.broadcast_to(row, (rows, rows)), 0.0), axis=1, keepdims=True)
 
-    def run_chunk(offsets):
-        blocks = [at(o) * 2 + k for o in offsets for k in range(2)]
+    def run_chunk(chips):
+        blocks = [chip * 2 + k for chip in chips for k in range(2)]
         count = len(blocks) * rows
         x = jnp.concatenate(
             [jnp.concatenate([X[0, b], X[1, b]], axis=1) for b in blocks], axis=0
@@ -476,136 +430,125 @@
             for k, b in enumerate(blocks):
                 P_ref[b, :, cols] = y[k * rows : (k + 1) * rows]
 
-        def tiled(body, total, tile):
-            whole_tiles = total // tile
-
-            @pl.loop(0, whole_tiles)
-            def _(i):
-                body(pl.multiple_of(i * tile, tile), tile)
-
-            if total % tile:
-                body(whole_tiles * tile, total % tile)
-
-        return tiled, first, second
-
-    order = [0]
-    for s in range(1, half_ring):
-        order += [-s, s]
-    order += [half_ring]
-    chunks = [order[k : k + 2] for k in range(0, len(order), 2)]
-
-    c_copies = []
-
-    def swap(offset):
-        dest = at(offset)
-        k = offset % rings
+        return first, second
+
+    def tiled(body, total, tile, start, stop):
+        whole_tiles = total // tile
+
+        @pl.loop(start, min(stop, whole_tiles))
+        def _(i):
+            body(pl.multiple_of(i * tile, tile), tile)
+
+        if total % tile and stop > whole_tiles:
+            body(whole_tiles * tile, total % tile)
+
+    tile = 256
+    first_tiles = -(-width // tile)
+    second_tiles = -(-2 * width // tile)
+
+    def swap(chip, k):
         copy = pltpu.make_async_remote_copy(
-            src_ref=P_ref.at[dest * 2 + 1 - c],
-            dst_ref=CS.at[dest],
+            src_ref=P_ref.at[chip * 2 + 1 - c],
+            dst_ref=CS.at[chip],
             send_sem=csend.at[k],
-            recv_sem=crecv.at[dest],
+            recv_sem=crecv.at[chip],
             device_id=mate,
             device_id_type=MESH,
         )
         copy.start()
         return copy
 
-    for step in range(1, half_ring + 1):
-        for h in halves:
-            forward(step, h)
-    for step in range(0, half_ring + 1):
-        for h in halves:
-            mates(step, h)
-    loads[0].wait()
-    loads[1].wait()
-    loads[2].wait()
-    swaps = {}
-    for offsets in chunks[::-1]:
-        tiled, first, second = run_chunk(offsets)
-        tiled(first, width, 256)
-        tiled(second, 2 * width, 256)
-        for o in offsets:
-            swaps[o % rings] = swap(o)
-
-    def chip_sum(offset):
-        dest = at(offset)
-        return P_ref[dest * 2 + c].astype(jnp.float32) + CS[dest].astype(jnp.float32)
-
-    ring_copies = []
-
-    def ring_copy(src, dst, k, d, target):
+    def halve(chip, k, swapped):
+        swapped.wait()
+        total = P_ref[chip * 2 + c].astype(jnp.float32) + CS[chip].astype(jnp.float32)
+        low, high = total[:, :width], total[:, width:]
+        KEEP[chip] = jnp.where(a == 0, low, high)
+        YS[chip] = jnp.where(a == 0, high, low).astype(jnp.bfloat16)
         copy = pltpu.make_async_remote_copy(
-            src_ref=src,
-            dst_ref=dst,
-            send_sem=rsend.at[k, d - 1],
-            recv_sem=rrecv.at[k, d - 1],
-            device_id=target,
+            src_ref=YS.at[chip],
+            dst_ref=YR.at[chip],
+            send_sem=ysend.at[k],
+            recv_sem=yrecv.at[chip],
+            device_id=across,
             device_id_type=MESH,
         )
         copy.start()
-        ring_copies.append(copy)
         return copy
 
-    coming = {}
-    lo = pl.ds(0, half_rows)
-    hi = pl.ds(half_rows, half_rows)
-    swapped = set()
-
-    def swap_done(offset):
-        k = offset % rings
-        if k not in swapped:
-            swapped.add(k)
-            swaps[k].wait()
-
-    for d in range(half_ring, 0, -1):
-        swap_done(d)
-        swap_done(-d)
-        if d == half_ring:
-            total = chip_sum(d).astype(jnp.bfloat16)
-            SR[d - 1, lo] = total[:half_rows]
-            SL[d - 1, hi] = total[half_rows:]
-            coming[0] = ring_copy(SR.at[d - 1, lo], RR.at[d - 1, lo], 0, d, right)
-            coming[1] = ring_copy(SL.at[d - 1, hi], RL.at[d - 1, hi], 1, d, left)
-            continue
-        if d + 1 == half_ring:
-            to_right = chip_sum(d)
-            to_left = chip_sum(-d)
-            coming[0].wait_recv()
-            SR[d - 1, lo] = (to_right[:half_rows] + RR[d, lo].astype(jnp.float32)).astype(jnp.bfloat16)
-            SR[d - 1, hi] = to_right[half_rows:].astype(jnp.bfloat16)
-            coming[0] = ring_copy(SR.at[d - 1], RR.at[d - 1], 0, d, right)
-            coming[1].wait_recv()
-            SL[d - 1, hi] = (to_left[half_rows:] + RL[d, hi].astype(jnp.float32)).astype(jnp.bfloat16)
-            SL[d - 1, lo] = to_left[:half_rows].astype(jnp.bfloat16)
-            coming[1] = ring_copy(SL.at[d - 1], RL.at[d - 1], 1, d, left)
+    def deliver(chip, k, halved):
+        halved.wait()
+        ZS[chip] = (KEEP[chip] + YR[chip].astype(jnp.float32)).astype(jnp.bfloat16)
+        copy = pltpu.make_async_remote_copy(
+            src_ref=ZS.at[chip],
+            dst_ref=ZR.at[z],
+            send_sem=rsend.at[k],
+            recv_sem=rrecv.at[z],
+            device_id={"exp": chip * 2 + c},
+            device_id_type=MESH,
+        )
+        copy.start()
+        pending.append(copy)
+
+    crossed(z)
+    pass_on(groups_of_chips[0][1])
+    crossed(groups_of_chips[0][1])
+    for chip in groups_of_chips[0]:
+        mates(chip)
+    loads[0].wait()
+    loads[1].wait()
+    halved = {}
+    position = 0
+    swaps = []
+    for number, chips in enumerate(groups_of_chips):
+        coming = groups_of_chips[number + 1] if number + 1 < pair_count else []
+        first, second = run_chunk(chips)
+        if coming:
+            tiled(first, width, tile, 0, 3)
+            pass_on(coming[0])
+            tiled(first, width, tile, 3, first_tiles)
+            pass_on(coming[1])
         else:
-            coming[0].wait_recv()
-            SR[d - 1] = (chip_sum(d) + RR[d].astype(jnp.float32)).astype(jnp.bfloat16)
-            coming[0] = ring_copy(SR.at[d - 1], RR.at[d - 1], 0, d, right)
-            coming[1].wait_recv()
-            SL[d - 1] = (chip_sum(-d) + RL[d].astype(jnp.float32)).astype(jnp.bfloat16)
-            coming[1] = ring_copy(SL.at[d - 1], RL.at[d - 1], 1, d, left)
-    swap_done(0)
-    total = chip_sum(0)
-    coming[0].wait_recv()
-    coming[1].wait_recv()
-    total = total + RR[0].astype(jnp.float32) + RL[0].astype(jnp.float32)
-    low, high = total[:, :width], total[:, width:]
-    mine = jnp.where(a == 0, low, high)
-    YS[...] = jnp.where(a == 0, high, low).astype(jnp.bfloat16)
-    last = pltpu.make_async_remote_copy(
-        src_ref=YS,
-        dst_ref=YR,
-        send_sem=ysend,
-        recv_sem=yrecv,
-        device_id=across,
-        device_id_type=MESH,
-    )
-    last.start()
-    for copy in pending + ring_copies:
+            tiled(first, width, tile, 0, first_tiles)
+        for chip, k, swapped in swaps:
+            halved[k] = (chip, halve(chip, k, swapped))
+        if number == 0:
+            loads[2].wait()
+        if coming:
+            tiled(second, 2 * width, tile, 0, second_tiles // 2)
+            crossed(coming[0])
+            tiled(second, 2 * width, tile, second_tiles // 2, second_tiles)
+            crossed(coming[1])
+        else:
+            tiled(second, 2 * width, tile, 0, second_tiles)
+        swaps = []
+        for chip in chips:
+            swaps.append((chip, position, swap(chip, position)))
+            position += 1
+        for k in list(halved):
+            if k > 0:
+                deliver(halved[k][0], k, halved.pop(k)[1])
+        for chip in coming:
+            mates(chip)
+    for chip, k, swapped in swaps:
+        halved[k] = (chip, halve(chip, k, swapped))
+    for k in sorted(halved):
+        if k > 0:
+            deliver(halved[k][0], k, halved[k][1])
+    halved[0][1].wait()
+    total = KEEP[z] + YR[z].astype(jnp.float32)
+    for chip in others:
+        pltpu.make_async_remote_copy(
+            src_ref=ZR.at[chip],
+            dst_ref=ZR.at[chip],
+            send_sem=rsend.at[0],
+            recv_sem=rrecv.at[chip],
+            device_id=mate,
+            device_id_type=MESH,
+        ).wait_recv()
+        total += ZR[chip].astype(jnp.float32)
+    out_ref[...] = total.astype(jnp.bfloat16)
+    for copy in pending:
         copy.wait_send()
-    last.wait()
-    out_ref[...] = (mine + YR[...].astype(jnp.float32)).astype(jnp.bfloat16)
 
 
 def layer(
@@ -613,7 +556,6 @@
 ):
     n = lax.axis_size("exp")
     rings = n // 2
-    half_ring = max(1, rings // 2)
     rows, width = residual.shape
     per = QUERY_HEADS // KEY_VALUE_HEADS
     pairs = KEY_VALUE_HEADS // 2
@@ -649,23 +591,22 @@
             pltpu.VMEM((per_chunk, width), bf),
             pltpu.VMEM((n, rows, full), bf),
             pltpu.VMEM((rings, rows, full), bf),
-            pltpu.VMEM((half_ring, rows, full), bf),
-            pltpu.VMEM((half_ring, rows, full), bf),
-            pltpu.VMEM((half_ring, rows, full), bf),
-            pltpu.VMEM((half_ring, rows, full), bf),
-            pltpu.VMEM((rows, width), bf),
-            pltpu.VMEM((rows, width), bf),
+            pltpu.VMEM((rings, rows, width), jnp.float32),
+            pltpu.VMEM((rings, rows, width), bf),
+            pltpu.VMEM((rings, rows, width), bf),
+            pltpu.VMEM((rings, rows, width), bf),
+            pltpu.VMEM((rings, rows, width), bf),
             dma((5,)),
             dma((sends,)),
-            dma((2, n, 2)),
+            dma((2, n)),
             dma((sends,)),
             dma((2, n)),
             dma((rings,)),
             dma((rings,)),
-            dma((2, half_ring)),
-            dma((2, half_ring)),
-            dma,
-            dma,
+            dma((rings,)),
+            dma((rings,)),
+            dma((rings,)),
+            dma((rings,)),
         ],
         compiler_params=pltpu.CompilerParams(
             collective_id=1, has_side_effects=True, vmem_limit_bytes=62 * 1024 * 1024

time: 121 us -> 105 us (0.87)
  Pallas kernels: 110 us -> 94.3 us
    pallas_call x1, Pallas kernels: 110 us -> 94.3 us  [layer(): pl.pallas_call(functools.partial(layer_kernel, n), out_shape=[jax.ShapeDt...]
where the time goes in v3:
time: 105 us
  Pallas kernels  94.3 us (90%)
  local copies, waits for them, and re-layouts  7.32 us (7%)
  other arithmetic  2.66 us (3%)
    pallas_call x1, Pallas kernels, layer(): pl.pallas_call(functools.partial(layer_kernel, n), out_shape=[jax.ShapeDt...  94.3 us
    unnamed x2, local copies, waits for them, and re-layouts  3.23 us

profile of v3, /device:TPU:0, one launch (start us, length us, event | category | flops | bytes accessed | tf_op | source)
XLA Modules:
  0.0 105.0 jit_solution(2830499652411188695)
XLA Ops:
  0.6 0.7 convert_reduce_fusion
  1.3 0.7 convert_divide_fusion
  2.0 1.3 %select_reduce_fusion.share_ref = f32[8,64]{1,0:T(8,128)} fusion(f32[64,4]{0,1:T(4,128)S(1)} %convert_divide_fusion, s32[64,4]{0,1:T(4,128)} %param.21), kind=kLoop, calls=%fused_computation | loop fusion | flops 5632 | bytes 4096 | tf_op jit(solution)/shard_map/reduce_sum | solution.py:634
  3.3 0.7 tile.2
  3.9 0.6 broadcast_in_dim_tile.3.branch_ref
  4.6 0.7 broadcast_in_dim.26
  5.3 1.3 %broadcast_in_dim.29.gain_ref = bf16[1,1440]{1,0:T(2,128)(2,1)} reshape(bf16[1440]{0:T(1024)(128)(2,1)} %param.20) | data formatting | bytes 5760 | tf_op jit(solution)/shard_map/broadcast_in_dim | solution.py:620
  6.6 0.1 broadcast_in_dim.27
  6.7 0.7 broadcast_in_dim.28.sink_ref
  7.4 94.3 %shard_map.140 = (bf16[64,1440]{1,0:T(8,128)(2,1)}, bf16[64,1440]{1,0:T(8,128)(2,1)}) custom-call(bf16[64,4096]{1,0:T(8,128)(2,1)} %q_ref.1, bf16[64,1024]{1,0:T(8,128)(2,1)} %kv_ref.1, s32[1,512]{1,0:T(1,128)} %broadcast_in_dim_tile.3.branch_ref, f32[4,2,512]{2,1,0:T(2,128)} %broadcast_in_dim.28.sink_ref, bf16[64,1440]{1,0:T(8,128)(2,1)} %residual_ref.1, ...), custom_call_target="tpu_custom_call" | custom-call | tf_op jit(solution)/shard_map/pallas_call | solution.py:568
  101.7 1.6 %copy.19 = bf16[64,1440]{1,0:T(8,128)(2,1)} copy(bf16[64,1440]{1,0:T(8,128)(2,1)} %get-tuple-element.4) | data formatting | bytes 368640
  103.3 1.6 %copy.20 = bf16[64,1440]{1,0:T(8,128)(2,1)} copy(bf16[64,1440]{1,0:T(8,128)(2,1)} %get-tuple-element.5) | data formatting | bytes 368640

commit v4 on v3

--- a/solution.py
+++ b/solution.py
@@ -140,7 +140,8 @@
     sink_ref,
     residual_ref,
     gain_ref,
-    share_ref,
+    ids_ref,
+    codes_ref,
     cache_hbm,
     wo_hbm,
     wg_hbm,
@@ -187,7 +188,7 @@
     rings = n // 2
     rows = residual_ref.shape[0]
     width = residual_ref.shape[1]
-    experts = share_ref.shape[0]
+    experts = META.shape[2]
     a = lax.axis_index("att")
     e = lax.axis_index("exp")
     z = e // 2
@@ -228,7 +229,7 @@
     pair = 2 * HEAD_SIZE
     pairs = KEY_VALUE_HEADS // 2
     kv_width = KEY_VALUE_HEADS * HEAD_SIZE
-    second_context = branch_ref[...] == 1
+    second_context = jnp.concatenate([branch_ref[...]] * per, axis=1) == 1
 
     def transposed_queries(g2):
         start = pl.multiple_of(g2 * 2 * per * HEAD_SIZE, 128)
@@ -304,7 +305,6 @@
         value_cols = pl.ds(pl.multiple_of(kv_width + g2 * pair, 128), pair)
         own_keys = kv_ref[:, key_cols].astype(jnp.float32).T
         own_values = kv_ref[:, value_cols].astype(jnp.float32).T
-        sinks = sink_ref[g2]
         for copy in parts_copies(g2):
             copy.wait()
         mine, theirs = TS[g2], TR[g2]
@@ -314,7 +314,9 @@
             own_key = jnp.concatenate([own_keys[own_rows]] * per, axis=1)
             own_value = jnp.concatenate([own_values[own_rows]] * per, axis=1)
             own_score = jnp.sum(heads_t[j] * own_key, axis=0, keepdims=True)
-            sink = sinks[j : j + 1]
+            sink = jnp.concatenate(
+                [jnp.full((1, rows), sink_ref[(g2 * 2 + j) * per + h]) for h in range(per)], axis=1
+            )
             top_a, top_b = mine[2 * j : 2 * j + 1], theirs[2 * j : 2 * j + 1]
             peak = jnp.maximum(jnp.maximum(top_a, top_b), jnp.maximum(own_score, sink))
             factor_a = jnp.exp(top_a - peak)
@@ -342,8 +344,14 @@
     squares = jnp.sum(
         jnp.where(eye, jnp.broadcast_to(squares, (rows, rows)), 0.0), axis=0, keepdims=True
     )
+    codes = codes_ref[...].astype(jnp.float32)
+    codes = codes / jnp.sum(codes, axis=0, keepdims=True)
+    row_of = lax.broadcasted_iota(jnp.int32, (experts, rows), 0)
+    table = jnp.zeros((experts, rows), jnp.float32)
+    for k in range(TOP):
+        table += jnp.where(row_of == ids_ref[k : k + 1, :], codes[k : k + 1, :], 0.0)
     META[a, e] = jnp.concatenate(
-        [share_ref[...], jnp.broadcast_to(squares, (experts, rows))], axis=1
+        [table, jnp.broadcast_to(squares, (experts, rows))], axis=1
     )
     X[a, e] = (hidden * gain_ref[...].astype(jnp.float32)).astype(jnp.bfloat16)
 
@@ -377,7 +385,8 @@
             ).wait_recv()
 
     send(a, e, across)
-    for chip in others:
+    twin, far, farther = others
+    for chip in (twin, far):
         send(a, e, {"exp": chip * 2 + c})
     send(a, e, mate)
 
@@ -385,6 +394,8 @@
         idx = chip * 2 + c
         arrived(a, idx)
         send(a, idx, across)
+        if chip is far:
+            send(a, idx, {"exp": twin * 2 + c})
         send(a, idx, mate)
 
     def crossed(chip):
@@ -475,15 +486,29 @@
         copy.start()
         return copy
 
-    def deliver(chip, k, halved):
+    def landed(slot):
+        pltpu.make_async_remote_copy(
+            src_ref=ZR.at[slot],
+            dst_ref=ZR.at[slot],
+            send_sem=rsend.at[0],
+            recv_sem=rrecv.at[slot],
+            device_id=mate,
+            device_id_type=MESH,
+        ).wait_recv()
+        return ZR[slot].astype(jnp.float32)
+
+    def deliver(chip, k, halved, target, slot):
         halved.wait()
-        ZS[chip] = (KEEP[chip] + YR[chip].astype(jnp.float32)).astype(jnp.bfloat16)
+        total = KEEP[chip] + YR[chip].astype(jnp.float32)
+        if chip is far:
+            total += landed(farther)
+        ZS[chip] = total.astype(jnp.bfloat16)
         copy = pltpu.make_async_remote_copy(
             src_ref=ZS.at[chip],
-            dst_ref=ZR.at[z],
+            dst_ref=ZR.at[slot],
             send_sem=rsend.at[k],
-            recv_sem=rrecv.at[z],
-            device_id={"exp": chip * 2 + c},
+            recv_sem=rrecv.at[slot],
+            device_id={"exp": target * 2 + c},
             device_id_type=MESH,
         )
         copy.start()
@@ -521,38 +546,26 @@
         else:
             tiled(second, 2 * width, tile, 0, second_tiles)
         swaps = []
-        for chip in chips:
+        for chip in chips if number == 0 else chips[::-1]:
             swaps.append((chip, position, swap(chip, position)))
             position += 1
-        for k in list(halved):
-            if k > 0:
-                deliver(halved[k][0], k, halved.pop(k)[1])
+        if 1 in halved:
+            deliver(twin, 1, halved[1][1], twin, z)
         for chip in coming:
             mates(chip)
     for chip, k, swapped in swaps:
         halved[k] = (chip, halve(chip, k, swapped))
-    for k in sorted(halved):
-        if k > 0:
-            deliver(halved[k][0], k, halved[k][1])
+    deliver(farther, 2, halved[2][1], twin, far)
+    deliver(far, 3, halved[3][1], far, z)
     halved[0][1].wait()
-    total = KEEP[z] + YR[z].astype(jnp.float32)
-    for chip in others:
-        pltpu.make_async_remote_copy(
-            src_ref=ZR.at[chip],
-            dst_ref=ZR.at[chip],
-            send_sem=rsend.at[0],
-            recv_sem=rrecv.at[chip],
-            device_id=mate,
-            device_id_type=MESH,
-        ).wait_recv()
-        total += ZR[chip].astype(jnp.float32)
+    total = KEEP[z] + YR[z].astype(jnp.float32) + landed(twin) + landed(far)
     out_ref[...] = total.astype(jnp.bfloat16)
     for copy in pending:
         copy.wait_send()
 
 
 def layer(
-    queries, row_key_value, cache, branch, sinks, w_out, residual, gain, by_expert, w_gate, w_up, w_down
+    queries, row_key_value, cache, branch, sinks, w_out, residual, gain, expert_ids, weight_codes, w_gate, w_up, w_down
 ):
     n = lax.axis_size("exp")
     rings = n // 2
@@ -560,7 +573,7 @@
     per = QUERY_HEADS // KEY_VALUE_HEADS
     pairs = KEY_VALUE_HEADS // 2
     full = 2 * width
-    experts = by_expert.shape[0]
+    experts = w_gate.shape[0] * n
     per_chunk = 4 * rows
     sends = 4 * n + 8
     bf = jnp.bfloat16
@@ -568,7 +581,9 @@
     return pl.pallas_call(
         functools.partial(layer_kernel, n),
         out_shape=[jax.ShapeDtypeStruct((rows, width), bf)] * 2,
-        in_specs=[pl.BlockSpec(memory_space=pltpu.VMEM)] * 7
+        in_specs=[pl.BlockSpec(memory_space=pltpu.VMEM)] * 3
+        + [pl.BlockSpec(memory_space=pltpu.SMEM)]
+        + [pl.BlockSpec(memory_space=pltpu.VMEM)] * 4
         + [pl.BlockSpec(memory_space=pl.ANY)] * 5,
         out_specs=[pl.BlockSpec(memory_space=pltpu.VMEM)] * 2,
         scratch_shapes=[
@@ -614,24 +629,18 @@
     )(
         queries,
         row_key_value,
-        jnp.tile(branch, per)[None, :],
-        jnp.repeat(sinks, rows).reshape(pairs, 2, per * rows),
+        branch[None, :],
+        sinks,
         residual,
         gain[None, :],
-        by_expert,
+        expert_ids.T,
+        weight_codes.T,
         cache,
         w_out.T,
         jnp.swapaxes(w_gate, 1, 2),
         jnp.swapaxes(w_up, 1, 2),
         w_down,
     )
-
-
-def share_table(expert_ids, weight_codes, expert_count):
-    shares = weight_codes.astype(jnp.float32)
-    shares = shares / jnp.sum(shares, axis=1, keepdims=True)
-    named = expert_ids[None, :, :] == jnp.arange(expert_count, dtype=jnp.int32)[:, None, None]
-    return jnp.sum(jnp.where(named, shares[None], 0.0), axis=2)
 
 
 def routed_experts(hidden, norm_gain, expert_ids, weight_codes, w_gate, w_up, w_down):
@@ -701,7 +710,7 @@
     w_up,
     w_down,
 ):
-    near = lax.axis_size("att") == 2 and lax.axis_size("exp") % 4 == 0 and w_gate.shape[0] == 1
+    near = lax.axis_size("att") == 2 and lax.axis_size("exp") == 8 and w_gate.shape[0] == 1
     if near:
         return layer(
             queries,
@@ -712,7 +721,8 @@
             w_out,
             residual,
             norm_gain,
-            share_table(expert_ids, weight_codes, w_gate.shape[0] * lax.axis_size("exp")),
+            expert_ids,
+            weight_codes,
             w_gate,
             w_up,
             w_down,

time: 105 us -> 96.6 us (0.920); the launches traced: 105 us -> 95.4 us
  Pallas kernels: 94.3 us -> 90.2 us
  local copies, waits for them, and re-layouts: 7.32 us -> 4.52 us
  other arithmetic: 2.66 us -> 0 us
    pallas_call x1, Pallas kernels: 94.3 us -> 90.2 us  [layer(): pl.pallas_call(functools.partial(layer_kernel, n), out_shape=[jax.ShapeDt...]
    reduce_sum x2 -> x0, other arithmetic: 1.98 us -> none  [the longest x1 1.28 us: share_table(): return jnp.sum(jnp.where(named, shares[None], 0.0), axis=2)]
    broadcast_in_dim x3 -> x0, local copies, waits for them, and re-layouts: 1.5 us -> none  [layer(): jnp.repeat(sinks, rows).reshape(pairs, 2, per * rows)]
    another operation x2 -> x0, local copies, waits for them, and re-layouts: 1.29 us -> none  [layer(): jnp.tile(branch, per)[None, :]]
where the time goes in v4:
time: 96.6 us; the launch traced here: 95.4 us
  Pallas kernels  90.2 us (93%)
  local copies, waits for them, and re-layouts  4.52 us (5%)
    pallas_call x1, Pallas kernels, layer(): pl.pallas_call(functools.partial(layer_kernel, n), out_shape=[jax.ShapeDt...  90.2 us
    unnamed x2, local copies, waits for them, and re-layouts  3.23 us

profile of v4, /device:TPU:0, one launch (start us, length us, event | category | flops | bytes accessed | tf_op | source)
XLA Modules:
  0.0 95.4 jit_solution(18248081680845739053)
XLA Ops:
  0.6 1.3 %broadcast_in_dim.7.gain_ref = bf16[1,1440]{1,0:T(2,128)(2,1)} reshape(bf16[1440]{0:T(1024)(128)(2,1)} %param.20) | data formatting | bytes 5760 | tf_op jit(solution)/shard_map/broadcast_in_dim | solution.py:635
  1.9 90.2 %shard_map.140 = (bf16[64,1440]{1,0:T(8,128)(2,1)}, bf16[64,1440]{1,0:T(8,128)(2,1)}) custom-call(bf16[64,4096]{1,0:T(8,128)(2,1)} %q_ref.1, bf16[64,1024]{1,0:T(8,128)(2,1)} %kv_ref.1, s32[1,64]{1,0:T(1,128)} %bitcast.11, f32[64]{0:T(128)} %sink_ref.1, bf16[64,1440]{1,0:T(8,128)(2,1)} %residual_ref.1, bf16[1,1440]{1,0:T(2,128)(2,1)} %broadcast_in_dim.7.gain_ref, ...), custom_call_target="tpu_custom_call" | custom-call | tf_op jit(solution)/shard_map/pallas_call | solution.py:581
  92.1 1.6 %copy.17 = bf16[64,1440]{1,0:T(8,128)(2,1)} copy(bf16[64,1440]{1,0:T(8,128)(2,1)} %get-tuple-element.4) | data formatting | bytes 368640
  93.7 1.6 %copy.18 = bf16[64,1440]{1,0:T(8,128)(2,1)} copy(bf16[64,1440]{1,0:T(8,128)(2,1)} %get-tuple-element.5) | data formatting | bytes 368640
